TPU v7x, 32 devices: a whole 2x2x4 slice. The times are simulated.
32 devices in a mesh: bins: 4 (over y, core), space: 8 (over z, x).
Axes of the slice: x: 2, y: 2, z: 4, core: 2. Of those that a mesh axis runs over, the one named last changes fastest.
Arguments:
- spectra: float32 [1152, 512, 128], P('bins', 'space'), may hold values from 0.05 to 2
- land_mask: int32 [512, 128], P('space'), may hold values 0 or 1
- growth: float32 [1152], replicated, may hold values from 0.1 to 1
- band_weight: float32 [1152], replicated, may hold values from 0.00043402778 to 0.0034722222
- kernel_gain: bfloat16 [1152, 1152], replicated, may hold values from -0.1875 to 0.1875
- kernel_loss: bfloat16 [1152, 1152], replicated, may hold values from -0.1875 to 0.1875
Outputs:
- updated: float32 [1152, 512, 128], P('bins', 'space')
All inputs are finite; a program needn't handle non-finite values. No bound on the sum of `land_mask` on one device may be relied on, other than what follows from the above.
Results may differ from a plain program's by a relative error of at most 0.00056.
Values sent between devices are 32-bit elements; how exact they have to be, the bound alone decides.
No kernel may reach another device: no remote copies, remote signals or barrier semaphores. Data moves between devices by JAX's collectives and lax.ppermute only.
A program may use at most 64 MiB of HBM per device.

v0:
```python
import functools
import math

import jax
import jax.numpy as jnp
import numpy as np
from jax import lax
from jax.experimental import pallas as pl
from jax.experimental.pallas import tpu as pltpu
from jax.sharding import PartitionSpec as P


NF = 32
ND = 36
SUBSTEPS = 4
TILE = 8
LANES = 128


def courants(first, count):
    index = first + jnp.arange(count, dtype=jnp.int32)
    freq = (index // ND).astype(jnp.float32)
    direc = (index % ND).astype(jnp.float32)
    group = 1.0 / (1.0 + 2.3 * freq / max(NF - 1, 1))
    theta = 2.0 * math.pi * (direc + 0.5) / ND
    return (0.9 * group * jnp.cos(theta), 0.9 * group * jnp.sin(theta))


def edge_kernel(low_ref, high_ref, low_mask, high_mask, head_ref, tail_ref):
    bins = low_ref.shape[0]
    low = low_ref.reshape(bins * TILE, LANES)
    high = high_ref.reshape(bins * TILE, LANES)
    for row in range(SUBSTEPS):
        behind = TILE - SUBSTEPS + row
        head_ref[row, pl.ds(0, bins), :] = low[pl.ds(row, bins, stride=TILE), :]
        tail_ref[row, pl.ds(0, bins), :] = high[pl.ds(behind, bins, stride=TILE), :]
        sea_low = low_mask[pl.ds(row, 1), :].astype(jnp.float32)
        sea_high = high_mask[pl.ds(behind, 1), :].astype(jnp.float32)
        head_ref[row, pl.ds(bins, TILE), :] = jnp.broadcast_to(sea_low, (TILE, LANES))
        tail_ref[row, pl.ds(bins, TILE), :] = jnp.broadcast_to(sea_high, (TILE, LANES))


def edges(spectra, land_mask):
    bins, rows, columns = spectra.shape
    last = rows // TILE - 1
    shape = jax.ShapeDtypeStruct((SUBSTEPS, bins + TILE, columns), jnp.float32)
    whole = pl.BlockSpec((SUBSTEPS, bins + TILE, columns), lambda i: (0, 0, 0))
    return pl.pallas_call(
        edge_kernel,
        grid=(1,),
        in_specs=[
            pl.BlockSpec((bins, TILE, columns), lambda i: (0, 0, 0)),
            pl.BlockSpec((bins, TILE, columns), lambda i: (0, last, 0)),
            pl.BlockSpec((TILE, columns), lambda i: (0, 0)),
            pl.BlockSpec((TILE, columns), lambda i: (last, 0)),
        ],
        out_specs=[whole, whole],
        out_shape=[shape, shape],
        name="edges",
    )(spectra, spectra, land_mask, land_mask)


def fill_sea(first, last, prev_mask, mid_mask, next_mask, halo_mask, sea_scr):
    for k in range(TILE + 2 * SUBSTEPS):
        if k < SUBSTEPS:
            if first:
                row = halo_mask[k, pl.ds(0, 1), :]
            else:
                row = prev_mask[pl.ds(TILE - SUBSTEPS + k, 1), :].astype(jnp.float32)
        elif k < SUBSTEPS + TILE:
            row = mid_mask[pl.ds(k - SUBSTEPS, 1), :].astype(jnp.float32)
        elif last:
            row = halo_mask[k - SUBSTEPS - TILE, pl.ds(0, 1), :]
        else:
            row = next_mask[pl.ds(k - SUBSTEPS - TILE, 1), :].astype(jnp.float32)
        sea_scr[k] = jnp.broadcast_to(row, (TILE, LANES))


def general_body(first, last, prev_ref, mid_ref, next_ref, halo_ref, cx_ref, cy_ref, sea_scr, target):
    bins = mid_ref.shape[0]
    window = TILE + 2 * SUBSTEPS
    mid = mid_ref.reshape(bins * TILE, LANES)
    before = None if first else prev_ref.reshape(bins * TILE, LANES)
    after = None if last else next_ref.reshape(bins * TILE, LANES)
    lane = lax.broadcasted_iota(jnp.int32, (TILE, LANES), 1)

    def body(tile, carry):
        base = pl.multiple_of(tile * TILE, TILE)
        origin = tile * (TILE * TILE)
        cx = cx_ref[pl.ds(base, TILE), :]
        cy = cy_ref[pl.ds(base, TILE), :]
        ax = jnp.abs(cx)
        ay = jnp.abs(cy)
        east = cx > 0.0
        from_left = (cy > 0.0) & (lane > 0)
        from_right = (cy <= 0.0) & (lane < LANES - 1)

        def load(k):
            if k < SUBSTEPS:
                if first:
                    return halo_ref[k, pl.ds(base, TILE), :]
                return before[pl.ds(origin + TILE - SUBSTEPS + k, TILE, stride=TILE), :]
            if k < SUBSTEPS + TILE:
                return mid[pl.ds(origin + k - SUBSTEPS, TILE, stride=TILE), :]
            if last:
                return halo_ref[k - SUBSTEPS - TILE, pl.ds(base, TILE), :]
            return after[pl.ds(origin + k - SUBSTEPS - TILE, TILE, stride=TILE), :]

        field = [load(k) for k in range(window)]
        for step in range(SUBSTEPS):
            start = step + 1
            fresh = []
            for k in range(start, window - start):
                here = k - step
                value = field[here]
                source = jnp.where(east, field[here - 1], field[here + 1])
                value = value - ax * (value - source)
                left = pltpu.roll(value, 1, 1)
                right = pltpu.roll(value, LANES - 1, 1)
                source = jnp.where(from_left, left, jnp.where(from_right, right, 0.0))
                value = value - ay * (value - source)
                fresh.append(sea_scr[k] * value)
            field = fresh
        for row in range(TILE):
            target[row, pl.ds(base, TILE), :] = field[row]
        return carry

    lax.fori_loop(0, bins // TILE, body, 0)


def quadrant_body(quadrant, first, last, mid_ref, outer_ref, halo_ref, unit_ref, me_ref, sea_scr, target, turns):
    octet, quarter = mid_ref.shape[:2]
    flat = octet * quarter * TILE
    mid = mid_ref.reshape(flat, LANES)
    outer = outer_ref.reshape(flat, LANES)
    lane = lax.broadcasted_iota(jnp.int32, (TILE, LANES), 1)
    east = quadrant in (0, 3)
    north = quadrant in (0, 1)
    edge = lane == (0 if north else LANES - 1)
    beyond = first if east else last
    skip = TILE - SUBSTEPS if east else 0
    octave = me_ref[0] * octet + lax.broadcasted_iota(jnp.int32, (TILE, LANES), 0)
    speed = 0.9 * (1.0 / (1.0 + 2.3 * octave.astype(jnp.float32) / max(NF - 1, 1)))

    def body(turn, carry):
        direction = quadrant * quarter + turn
        comb = pl.ds(direction, TILE, stride=ND)

        def cells(ref, row):
            return ref[pl.ds(turn * TILE + row, TILE, stride=quarter * TILE), :]

        ax = speed * unit_ref[0, direction]
        ay = speed * unit_ref[1, direction]
        stay = 1.0 - ax
        keep = 1.0 - ay
        take = jnp.where(edge, 0.0, ay)
        inner = [cells(mid, row) for row in range(TILE)]
        if beyond:
            upwind = [halo_ref[row, comb, :] for row in range(SUBSTEPS)]
        else:
            upwind = [cells(outer, skip + row) for row in range(SUBSTEPS)]
        field = upwind + inner if east else inner + upwind
        for step in range(SUBSTEPS):
            fresh = []
            for k in range(len(field) - 1):
                if east:
                    value, source, at = field[k + 1], field[k], step + 1 + k
                else:
                    value, source, at = field[k], field[k + 1], SUBSTEPS + k
                value = stay * value + ax * source
                aside = pltpu.roll(value, 1 if north else LANES - 1, 1)
                fresh.append(sea_scr[at] * (keep * value + take * aside))
            field = fresh
        for row in range(TILE):
            target[row, comb, :] = field[row]
        return carry

    lax.fori_loop(0, quarter, body, 0, unroll=turns)


def by_quadrant(bins):
    return bins == TILE * ND and ND % 4 == 0


def advance(first, last, cells, halo_ref, masks, halo_mask, speeds, sea_scr, target, turns=ND // 4):
    part = pl.program_id(1)

    @pl.when(part == 0)
    def _():
        fill_sea(first, last, *masks, halo_mask, sea_scr)

    if len(cells) == 3:
        general_body(first, last, *cells, halo_ref, *speeds, sea_scr, target)
        return
    for quadrant in range(4):

        @pl.when(part == quadrant)
        def _(quadrant=quadrant):
            quadrant_body(quadrant, first, last, *cells, halo_ref, *speeds, sea_scr, target, turns)


def cell_inputs(spectra, land_mask, at):
    bins, rows, columns = spectra.shape
    last_block = rows // TILE - 1

    def near(shift):
        return lambda i, *p: jnp.clip(at(i, *p) + shift, 0, last_block)

    if by_quadrant(bins):
        whole = spectra.reshape(TILE, ND, rows, columns)
        shape = (TILE, ND // 4, TILE, columns)

        def upwind(i, q, *p):
            shift = jnp.where((q == 0) | (q == 3), -1, 1)
            return (0, q, jnp.clip(at(i, *p) + shift, 0, last_block), 0)

        specs = [pl.BlockSpec(shape, lambda i, q, *p: (0, q, at(i, *p), 0)), pl.BlockSpec(shape, upwind)]
        args = [whole] * 2
        parts = 4
    else:
        shape = (bins, TILE, columns)
        specs = [pl.BlockSpec(shape, lambda i, q, *p, f=near(k): (0, f(i, *p), 0)) for k in (-1, 0, 1)]
        args = [spectra] * 3
        parts = 1
    specs += [pl.BlockSpec((TILE, columns), lambda i, q, *p, f=near(k): (f(i, *p), 0)) for k in (-1, 0, 1)]
    return specs, args + [land_mask] * 3, parts


def speed_inputs(bins, columns, me):
    if by_quadrant(bins):
        theta = 2.0 * np.pi * (np.arange(ND) + 0.5) / ND
        units = np.abs(np.stack([np.cos(theta), np.sin(theta)])).astype(np.float32)
        specs = [pl.BlockSpec(memory_space=pltpu.SMEM)] * 2
        return specs, [jnp.asarray(units), me.reshape(1)]
    speeds = courants(me * bins, bins)
    specs = [pl.BlockSpec((bins, columns), lambda *_: (0, 0))] * 2
    return specs, [jnp.broadcast_to(c[:, None], (bins, columns)) for c in speeds]


def propagate_kernel(first, last, cells, turns, _, *refs):
    fields, masks, rest = refs[:cells], refs[cells : cells + 3], refs[cells + 3 :]
    halo_ref = halo_mask = None
    if first or last:
        halo_ref, halo_mask, rest = rest[0], rest[1], rest[2:]
    *speeds, out_ref, sea_scr = rest
    advance(first, last, fields, halo_ref, masks, halo_mask, speeds, sea_scr, out_ref, turns)


def propagate(spectra, land_mask, speeds, block, halo=None, first=False, turns=ND // 4):
    bins, _, columns = spectra.shape
    last = halo is not None and not first
    specs, args, parts = cell_inputs(spectra, land_mask, lambda i, p: p[0])
    cells = len(args) - 3
    if first or last:
        specs.append(pl.BlockSpec((SUBSTEPS, bins, columns), lambda *_: (0, 0, 0)))
        specs.append(pl.BlockSpec((SUBSTEPS, TILE, columns), lambda *_: (0, bins // TILE, 0)))
        args += [halo, halo]
    return pl.pallas_call(
        functools.partial(propagate_kernel, first, last, cells, turns),
        grid_spec=pltpu.PrefetchScalarGridSpec(
            num_scalar_prefetch=1,
            grid=(1, parts),
            in_specs=specs + speeds[0],
            out_specs=pl.BlockSpec((TILE, bins, columns), lambda *_: (0, 0, 0)),
            scratch_shapes=[pltpu.VMEM((TILE + 2 * SUBSTEPS, TILE, columns), jnp.float32)],
        ),
        out_shape=jax.ShapeDtypeStruct((TILE, bins, columns), jnp.float32),
        name="propagate",
    )(jnp.full((1,), block, jnp.int32), *args, *speeds[1])


PAIR = 2


def source_kernel(count, aliased, where_ref, _, *refs):
    fields = refs[:count]
    gain_ref, loss_ref, growth_ref, weight_ref, mask_ref = refs[count : count + 5]
    rest = refs[count + 5 :]
    if aliased:
        rest = rest[1:]
    out_ref, state, square = rest
    bins = fields[0].shape[1]
    step = pl.program_id(0)
    energy = [jnp.zeros((TILE, LANES), jnp.float32) for _ in range(PAIR)]
    for n in range(count):
        place = pl.multiple_of(where_ref[n] * bins, 16)
        for row in range(PAIR):
            value = fields[n][row]
            state[pl.ds(place, bins), pl.ds(row * LANES, LANES)] = value.astype(jnp.bfloat16)
            square[pl.ds(place, bins), pl.ds(row * LANES, LANES)] = (value * value).astype(jnp.bfloat16)
            weighted = weight_ref[pl.ds(place, bins), :] * value
            energy[row] = energy[row] + jnp.sum(weighted.reshape(bins // TILE, TILE, LANES), axis=0)
    gain = jnp.dot(gain_ref[...], state[...], preferred_element_type=jnp.float32)
    loss = jnp.dot(loss_ref[...], square[...], preferred_element_type=jnp.float32)
    out = out_ref.reshape(bins * TILE, LANES)
    for row in range(PAIR):
        at = step * PAIR + row
        total = jnp.sum(energy[row], axis=0, keepdims=True)
        sea = mask_ref[pl.ds(at, 1), :].astype(jnp.float32)
        scale = sea / (1.0 + 0.5 * total)
        value = fields[0][row]
        grown = growth_ref[...] * value
        part = slice(row * LANES, (row + 1) * LANES)
        fresh = (value + 0.25 * (grown + value * gain[:, part] - loss[:, part])) * scale
        out[pl.ds(at, bins, stride=TILE), :] = fresh


def add_sources(where, fields, kernels, growth, weight, land_mask, block, out, shape):
    count = len(fields)
    bins, _, columns = shape
    every = weight.shape[0]
    cells = pl.BlockSpec((PAIR, bins, columns), lambda i, w, b: (i, 0, 0))
    table = pl.BlockSpec((bins, every), lambda i, w, b: (w[0], 0))
    specs = [cells] * count + [
        table,
        table,
        pl.BlockSpec((bins, columns), lambda i, w, b: (0, 0)),
        pl.BlockSpec((every, columns), lambda i, w, b: (0, 0)),
        pl.BlockSpec((TILE, columns), lambda i, w, b: (b[0], 0)),
    ]
    args = [*fields, *kernels, growth, weight, land_mask]
    aliases = {}
    if out is not None:
        specs.append(pl.BlockSpec(memory_space=pl.ANY))
        args.append(out)
        aliases = {len(args) + 1: 0}
    return pl.pallas_call(
        functools.partial(source_kernel, count, out is not None),
        grid_spec=pltpu.PrefetchScalarGridSpec(
            num_scalar_prefetch=2,
            grid=(TILE // PAIR,),
            in_specs=specs,
            out_specs=pl.BlockSpec((bins, TILE, columns), lambda i, w, b: (0, b[0], 0)),
            scratch_shapes=[
                pltpu.VMEM((every, PAIR * columns), jnp.bfloat16),
                pltpu.VMEM((every, PAIR * columns), jnp.bfloat16),
            ],
        ),
        out_shape=jax.ShapeDtypeStruct(shape, jnp.float32),
        input_output_aliases=aliases,
        name="sources",
    )(where, jnp.full((1,), block, jnp.int32), *args)


def plan_kernel(mask_ref, base_ref, order_ref, least_ref, room_ref, spot_ref, group_ref, over_ref):
    sea = mask_ref[...].astype(jnp.float32)
    marks = sea.astype(jnp.bfloat16)
    row = lax.broadcasted_iota(jnp.int32, (LANES, LANES), 0)
    lane = lax.broadcasted_iota(jnp.int32, (LANES, LANES), 1)
    ahead = (row < lane).astype(jnp.float32).astype(jnp.bfloat16)
    every = jnp.ones((LANES, LANES), jnp.bfloat16)
    rank = jnp.dot(marks, ahead, preferred_element_type=jnp.float32)
    count = jnp.dot(marks, every, preferred_element_type=jnp.float32)
    counts = count.astype(jnp.bfloat16)
    start = jnp.dot(base_ref[...], counts, preferred_element_type=jnp.float32)
    start = jnp.maximum(start, least_ref[...])
    start = start + jnp.dot(order_ref[...], counts, preferred_element_type=jnp.float32)
    group = lax.shift_right_logical(start.astype(jnp.int32), 7)
    spot = start.astype(jnp.int32) - group * LANES + rank.astype(jnp.int32)
    spot_ref[...] = jnp.where(sea > 0.0, spot, -1)
    group_ref[...] = group
    excess = jnp.max(start + count - room_ref[...], axis=0, keepdims=True)
    over_ref[...] = jnp.broadcast_to((excess > 0.0).astype(jnp.int32), (TILE, LANES))


def plan(land_mask, chunks):
    rows, columns = land_mask.shape
    base = np.zeros((rows, rows), np.float32)
    order = np.zeros((rows, rows), np.float32)
    least = np.zeros((rows, columns), np.float32)
    room = np.full((rows, columns), 2.0 * rows * columns, np.float32)
    for blocks, packed in chunks:
        if packed is None:
            continue
        for k, block in enumerate(blocks):
            own = np.arange(TILE * block, TILE * block + TILE)
            for earlier in blocks[:k]:
                base[own, TILE * earlier : TILE * earlier + TILE] = 1.0
            for row in own:
                order[row, own[0] : row] = 1.0
            room[own] = LANES * sum(packed)
            if 0 in blocks and block == 0:
                room[own] = LANES * sum(packed[:-1])
            if 0 in blocks and k == len(blocks) - 1:
                least[own] = LANES * sum(packed[:-2])
    table = jax.ShapeDtypeStruct((rows, columns), jnp.int32)
    small = jax.ShapeDtypeStruct((TILE, columns), jnp.int32)
    tables = (jnp.asarray(base, jnp.bfloat16), jnp.asarray(order, jnp.bfloat16), jnp.asarray(least), jnp.asarray(room))
    return pl.pallas_call(plan_kernel, out_shape=[table, table, small], name="plan")(land_mask, *tables)


def listed(blocks):
    def at(i, *_):
        block = blocks[0]
        for k, b in enumerate(blocks[1:], 1):
            block = jnp.where(i == k, b, block)
        return block

    return at


def pack_kernel(edge, blocks, packed, cells, group_ref, *refs):
    fields, masks, refs = refs[:cells], refs[cells : cells + 3], refs[cells + 3 :]
    if edge:
        before, before_mask, after, after_mask = refs[:4]
        refs = refs[4:]
    spot_ref, *speeds = refs[:3]
    outs = refs[3 : 3 + len(packed)]
    field, total, sea_scr = refs[3 + len(packed) :]
    step, part = pl.program_id(0), pl.program_id(1)
    steps, parts = pl.num_programs(0), pl.num_programs(1)
    room = sum(packed)

    @pl.when((step == 0) & (part == 0))
    def _():
        total[...] = jnp.zeros_like(total)

    first = blocks.index(0) if edge else -1
    last = len(blocks) - 1 if edge else -1

    @pl.when((step != first) & (step != last))
    def _():
        advance(False, False, fields, None, masks, None, speeds, sea_scr, field)

    if edge:

        @pl.when(step == first)
        def _():
            advance(True, False, fields, before, masks, before_mask, speeds, sea_scr, field)

        @pl.when(step == last)
        def _():
            advance(False, True, fields, after, masks, after_mask, speeds, sea_scr, field)

    slot = lax.broadcasted_iota(jnp.int32, (2 * LANES, LANES), 0)

    def gather(row, carry):
        at = jnp.minimum(group_ref[listed(blocks)(step) * TILE + row], room)
        spots = spot_ref[pl.ds(row, 1), :]
        pick = jnp.where(slot == spots, 1.0, 0.0).astype(jnp.bfloat16)
        value = field[row]
        high = value.astype(jnp.bfloat16)
        low = (value - high.astype(jnp.float32)).astype(jnp.bfloat16)
        both = jnp.concatenate([high, low], axis=1)
        picks = jnp.concatenate([pick, pick], axis=1)
        moved = lax.dot_general(both, picks, (((1,), (1,)), ((), ())), preferred_element_type=jnp.float32)
        total[at] = total[at] + moved[:, :LANES]
        total[at + 1] = total[at + 1] + moved[:, LANES:]
        return carry

    @pl.when(part == parts - 1)
    def _():
        lax.fori_loop(0, TILE, gather, 0, unroll=TILE)

    @pl.when((step == steps - 1) & (part == parts - 1))
    def _():
        start = 0
        for size, out in zip(packed, outs):
            for k in range(size):
                out[k] = total[start + k]
            start += size


def pack(spectra, land_mask, speeds, blocks, packed, groups, spots, halos):
    bins, _, columns = spectra.shape
    edge = halos is not None
    at = listed(blocks)
    specs, args, parts = cell_inputs(spectra, land_mask, at)
    cells = len(args) - 3
    if edge:
        wide = pl.BlockSpec((SUBSTEPS, bins, columns), lambda i, q, g: (0, 0, 0))
        sea = pl.BlockSpec((SUBSTEPS, TILE, columns), lambda i, q, g: (0, bins // TILE, 0))
        specs += [wide, sea, wide, sea]
        args += [halos[0], halos[0], halos[1], halos[1]]
    specs += [pl.BlockSpec((TILE, columns), lambda i, q, g: (at(i), 0))] + speeds[0]
    return pl.pallas_call(
        functools.partial(pack_kernel, edge, blocks, packed, cells),
        grid_spec=pltpu.PrefetchScalarGridSpec(
            num_scalar_prefetch=1,
            grid=(len(blocks), parts),
            in_specs=specs,
            out_specs=[pl.BlockSpec((n, bins, columns), lambda i, q, g: (0, 0, 0)) for n in packed],
            scratch_shapes=[
                pltpu.VMEM((TILE, bins, columns), jnp.float32),
                pltpu.VMEM((sum(packed) + 2, bins, columns), jnp.float32),
                pltpu.VMEM((TILE + 2 * SUBSTEPS, TILE, columns), jnp.float32),
            ],
        ),
        out_shape=[jax.ShapeDtypeStruct((n, bins, columns), jnp.float32) for n in packed],
        name="pack",
    )(groups, *args, spots, *speeds[1])


def packed_sources_kernel(count, size, where_ref, *refs):
    fields = refs[: PAIR * count]
    gain_ref, loss_ref, growth_ref, weight_ref, out_ref = refs[PAIR * count : PAIR * count + 5]
    state, square, gain, loss = refs[PAIR * count + 5 :]
    bins = fields[0].shape[1]
    step = pl.program_id(0)
    half = 2 * TILE

    energy = tuple(jnp.zeros((TILE, LANES), jnp.float32) for _ in range(PAIR))
    for n in range(count):
        place = pl.multiple_of(where_ref[n] * bins, half)

        def convert(tile, energy, n=n, place=place):
            base = pl.multiple_of(tile * half, half)
            to = pl.ds(pl.multiple_of(place + base, half), half)
            weight = weight_ref[to, :]
            fresh = []
            for k in range(PAIR):
                value = fields[PAIR * n + k][0, pl.ds(base, half), :]
                lanes = pl.ds(k * LANES, LANES)
                state[to, lanes] = value.astype(jnp.bfloat16)
                square[to, lanes] = (value * value).astype(jnp.bfloat16)
                weighted = weight * value
                fresh.append(energy[k] + weighted[:TILE] + weighted[TILE:])
            return tuple(fresh)

        energy = lax.fori_loop(0, bins // half, convert, energy, unroll=bins // half)
    gain[...] = jnp.dot(gain_ref[...], state[...], preferred_element_type=jnp.float32)
    loss[...] = jnp.dot(loss_ref[...], square[...], preferred_element_type=jnp.float32)
    scales = []
    for k in range(PAIR):
        total = jnp.sum(energy[k], axis=0, keepdims=True)
        scales.append(jnp.broadcast_to(1.0 / (1.0 + 0.5 * total), (TILE, LANES)))

    def finish(tile, carry):
        part = pl.ds(pl.multiple_of(tile * TILE, TILE), TILE)
        grow = growth_ref[part, :]
        for k in range(PAIR):
            value = fields[k][0, part, :]
            lanes = pl.ds(k * LANES, LANES)
            change = grow * value + value * gain[part, lanes] - loss[part, lanes]
            to = jnp.minimum(step * PAIR + k, size - 1)
            out_ref[to, part, :] = (value + 0.25 * change) * scales[k]
        return carry

    lax.fori_loop(0, bins // TILE, finish, 0, unroll=bins // TILE)


def packed_sources(where, fields, kernels, growth, weight):
    count = len(fields)
    size, bins, columns = fields[0].shape
    every = weight.shape[0]
    one = [
        pl.BlockSpec((1, bins, columns), lambda i, w, k=k: (jnp.minimum(i * PAIR + k, size - 1), 0, 0))
        for k in range(PAIR)
    ]
    table = pl.BlockSpec((bins, every), lambda i, w: (w[0], 0))
    specs = one * count + [
        table,
        table,
        pl.BlockSpec((bins, columns), lambda i, w: (0, 0)),
        pl.BlockSpec((every, columns), lambda i, w: (0, 0)),
    ]
    args = [f for field in fields for f in [field] * PAIR]
    return pl.pallas_call(
        functools.partial(packed_sources_kernel, count, size),
        grid_spec=pltpu.PrefetchScalarGridSpec(
            num_scalar_prefetch=1,
            grid=((size + PAIR - 1) // PAIR,),
            in_specs=specs,
            out_specs=pl.BlockSpec((size, bins, columns), lambda i, w: (0, 0, 0)),
            scratch_shapes=[
                pltpu.VMEM((every, PAIR * columns), jnp.bfloat16),
                pltpu.VMEM((every, PAIR * columns), jnp.bfloat16),
                pltpu.VMEM((bins, PAIR * columns), jnp.float32),
                pltpu.VMEM((bins, PAIR * columns), jnp.float32),
            ],
        ),
        out_shape=jax.ShapeDtypeStruct((size, bins, columns), jnp.float32),
        name="packed_sources",
    )(where, *args, *kernels, growth, weight)


def spread_kernel(base, packed, skip, group_ref, *refs):
    parts = refs[: len(packed)]
    spot_ref, _, out_ref, both = refs[len(packed) :]
    step = pl.program_id(0)
    bins = parts[0].shape[1]
    room = sum(packed)

    @pl.when(step == 0)
    def _():
        start = 0
        for size, part in zip(packed, parts):

            def split(k, carry, part=part, start=start):
                value = part[k]
                high = value.astype(jnp.bfloat16)
                both[start + k, :, :LANES] = high
                both[start + k, :, LANES:] = (value - high.astype(jnp.float32)).astype(jnp.bfloat16)
                return carry

            lax.fori_loop(0, size, split, 0)
            start += size

    slot = lax.broadcasted_iota(jnp.int32, (LANES, LANES), 0)
    out = out_ref.reshape(bins * TILE, LANES)
    for row in range(TILE):
        at = jnp.clip(group_ref[(base + step) * TILE + row] - skip, 0, room - 1)
        after = jnp.minimum(at + 1, room - 1)
        spots = spot_ref[pl.ds(row, 1), :]
        near = jnp.where(slot == spots, 1.0, 0.0).astype(jnp.bfloat16)
        far = jnp.where(slot + LANES == spots, 1.0, 0.0).astype(jnp.bfloat16)
        value = jnp.dot(both[at], jnp.concatenate([near, near], axis=0), preferred_element_type=jnp.float32)
        value = value + jnp.dot(both[after], jnp.concatenate([far, far], axis=0), preferred_element_type=jnp.float32)
        out[pl.ds(row, bins, stride=TILE), :] = value


def spread(parts, groups, spots, blocks, out, skip=0):
    bins, _, columns = out.shape
    packed = [p.shape[0] for p in parts]
    base = blocks[0]
    at = lambda i: base + i
    specs = [pl.BlockSpec((n, bins, columns), lambda i, g: (0, 0, 0)) for n in packed]
    specs += [pl.BlockSpec((TILE, columns), lambda i, g: (at(i), 0)), pl.BlockSpec(memory_space=pl.ANY)]
    return pl.pallas_call(
        functools.partial(spread_kernel, base, packed, skip),
        grid_spec=pltpu.PrefetchScalarGridSpec(
            num_scalar_prefetch=1,
            grid=(len(blocks),),
            in_specs=specs,
            out_specs=pl.BlockSpec((bins, TILE, columns), lambda i, g: (0, at(i), 0)),
            scratch_shapes=[pltpu.VMEM((sum(packed), bins, 2 * columns), jnp.bfloat16)],
        ),
        out_shape=jax.ShapeDtypeStruct(out.shape, jnp.float32),
        input_output_aliases={len(parts) + 2: 0},
        name="spread",
    )(groups, *parts, spots, out)


def layout(rows):
    last = rows // TILE - 1

    def room(blocks):
        points = len(blocks) * TILE * LANES
        return -(-points * 25 // (32 * LANES))

    inner = list(range(2, last))
    chunks = [([1], None)]
    while len(inner) > 2:
        blocks, inner = inner[:3], inner[3:]
        chunks.append((blocks, cut(room(blocks), 6)))
    edge = inner + [0, last]
    chunks.append((edge, cut(room(edge) - 12, 6) + [4, 4, 4]))
    return chunks


def cut(groups, size):
    pieces = max(groups // size, 1)
    return [groups // pieces + (k < groups % pieces) for k in range(pieces)]


def local(spectra, land_mask, growth, band_weight, kernel_gain, kernel_loss):
    bins, rows, columns = spectra.shape
    every = band_weight.shape[0]
    me = lax.axis_index("bins")
    group = lax.axis_size("bins")
    slabs = lax.axis_size("space")
    chips = group // 2
    last = rows // TILE - 1
    kernels = (kernel_gain, kernel_loss)
    partner = [(i, i ^ 1) for i in range(group)]
    shifts = [[(i, (i + 2 * s) % group) for i in range(group)] for s in range(1, chips)]
    chunks = layout(rows)

    speeds = speed_inputs(bins, columns, me)
    mine = lax.dynamic_slice_in_dim(growth, me * bins, bins)
    growth_wide = jnp.broadcast_to(mine[:, None], (bins, columns))
    weight_wide = jnp.broadcast_to(band_weight[:, None], (every, columns))
    came = [(me + group - 2 * s) % group for s in range(1, chips)]
    where = [me, me ^ 1]
    for source in came:
        where += [source, source ^ 1]
    where = jnp.stack(where).astype(jnp.int32)

    def exchange(piece):
        far = [lax.ppermute(piece, "bins", s) for s in shifts]
        near = lax.ppermute(piece, "bins", partner)
        parts = [piece, near]
        for came_in in far:
            parts += [came_in, lax.ppermute(came_in, "bins", partner)]
        return parts

    whole = propagate(spectra, land_mask, speeds, 1)
    gathered = [[exchange(whole)]]
    spots, group_rows, over = plan(land_mask, chunks)
    groups = group_rows[:, 0]
    head, tail = edges(spectra, land_mask)
    before = lax.ppermute(tail, "space", [(n, n + 1) for n in range(slabs - 1)])
    after = lax.ppermute(head, "space", [(n + 1, n) for n in range(slabs - 1)])
    reach = 1
    while reach < slabs:
        ring = [(n, (n + reach) % slabs) for n in range(slabs)]
        over = jnp.maximum(over, lax.ppermute(over, "space", ring))
        reach *= 2

    for c, (blocks, packed) in enumerate(chunks[1:], 1):
        halos = (before, after) if 0 in blocks else None
        pieces = pack(spectra, land_mask, speeds, blocks, packed, groups, spots, halos)
        gathered.append([])
        for piece in pieces:
            gathered[c].append(exchange(piece))

    out = add_sources(where, gathered[0][0], kernels, growth_wide, weight_wide, land_mask, 1, None, spectra.shape)
    for c, (blocks, packed) in enumerate(chunks[1:], 1):
        parts = []
        for fields in gathered[c]:
            parts.append(packed_sources(where, fields, kernels, growth_wide, weight_wide))
            if 0 in blocks and len(parts) == len(packed) - 2:
                out = spread(parts, groups, spots, blocks[:-2], out)
            if 0 in blocks and len(parts) == len(packed) - 1:
                crowded, parts[-1] = lax.optimization_barrier((over[0, 0] > 0, parts[-1]))
                out = spread(parts, groups, spots, [0], out)
        if 0 in blocks:
            out = spread(parts[-2:], groups, spots, [last], out, sum(packed[:-2]))
        else:
            out = spread(parts, groups, spots, blocks, out)

    def again(out):
        def redo(block, out, halo=None, first=False):
            field = propagate(spectra, land_mask, speeds, block, halo, first, 1)
            fields = [field, lax.ppermute(field, "bins", partner)]
            for s in shifts:
                came_in = lax.ppermute(field, "bins", s)
                fields += [came_in, lax.ppermute(came_in, "bins", partner)]
            return add_sources(
                where, fields, kernels, growth_wide, weight_wide, land_mask, block, out, spectra.shape
            )

        out = lax.fori_loop(2, last, redo, out)
        return redo(last, redo(0, out, before, True), after)

    return lax.cond(crowded, again, lambda out: out, out)


def solution(mesh):
    in_specs = (P("bins", "space", None), P("space", None), P(), P(), P(), P())
    out_specs = P("bins", "space", None)
    return jax.shard_map(local, mesh=mesh, in_specs=in_specs, out_specs=out_specs, check_vma=False)
```

profile of v0, /device:TPU:3, one launch (start us, length us, event | category | flops | bytes accessed | tf_op | source)
XLA Modules:
  0.0 293.8 jit_solution(13876953740843044585)
XLA Ops:
  0.0 1.7 plan.1
  1.7 1.4 slice_reduce_fusion.group_ref
  3.2 16.5 %pack.3 = (f32[7,288,128]{2,1,0:T(8,128)}, f32[6,288,128]{2,1,0:T(8,128)}, f32[6,288,128]{2,1,0:T(8,128)}) custom-call(s32[64]{0:T(128)} %slice_reduce_fusion.group_ref, f32[8,36,64,128]{3,2,1,0:T(8,128)} %bitcast.13, f32[8,36,64,128]{3,2,1,0:T(8,128)} %bitcast.14, s32[64,128]{1,0:T(8,128)} %refs_8_.17, s32[64,128]{1,0:T(8,128)} %refs_8_.17, ...), custom_call_target="tpu_custom_call" | custom-call | tf_op jit(solution)/shard_map/pack/pallas_call | solution.py:476
  19.6 1.3 collective-permute-start.33
  20.9 1.0 collective-permute-start.32
  21.9 2.9 edges.1
  24.8 3.2 %collective-permute-start.12 = (f32[4,296,128]{2,1,0:T(8,128)}, f32[4,296,128]{2,1,0:T(8,128)S(1)}, u32[]{:S(2)}, u32[]{:S(2)}) collective-permute-start(f32[4,296,128]{2,1,0:T(8,128)} %get-tuple-element.227), channel_id=1, source_target_pairs={{0,1},{1,2},{2,3},{3,4},{4,5},{5,6},{6,7},{8,9},{9,10},{10,11},{11... | collective-permute-start | bytes 1818632 | tf_op jit(solution)/shard_map/ppermute | solution.py:692
  27.9 2.1 collective-permute-start.13
  30.1 2.2 collective-permute-start.9
  32.3 22.9 %collective-permute-done.9 = s32[8,128]{1,0:T(8,128)S(1)} collective-permute-done((s32[8,128]{1,0:T(8,128)S(1)}, s32[8,128]{1,0:T(8,128)S(1)}, u32[]{:S(2)}, u32[]{:S(2)}) %collective-permute-start.9) | collective-permute-done | bytes 4128 | tf_op jit(solution)/shard_map/ppermute | solution.py:697
  55.2 1.3 collective-permute-start.10
  56.5 3.0 %collective-permute-done.10 = s32[8,128]{1,0:T(8,128)S(1)} collective-permute-done((s32[8,128]{1,0:T(8,128)S(1)}, s32[8,128]{1,0:T(8,128)S(1)}, u32[]{:S(2)}, u32[]{:S(2)}) %collective-permute-start.10) | collective-permute-done | bytes 4128 | tf_op jit(solution)/shard_map/ppermute | solution.py:697
  59.4 0.5 collective-permute-start.11
  60.0 2.8 collective-permute-done.11
  62.8 0.2 collective-permute-start.36
  63.0 5.4 %propagate.6.refs_0_ = f32[8,288,128]{2,1,0:T(8,128)} custom-call(s32[1]{0:T(128)} %constant.60.clone.1._, f32[8,36,64,128]{3,2,1,0:T(8,128)} %bitcast.15, f32[8,36,64,128]{3,2,1,0:T(8,128)} %bitcast.16, s32[64,128]{1,0:T(8,128)S(1)} %copy-done.1, s32[64,128]{1,0:T(8,128)S(1)} %copy-done.1, s32[64,128]{1,0:T(8,128)S(1)} %copy-done.1, ...), custom_call_target="tpu_custom_call" | custom-call | tf_op jit(solution)/shard_map/propagate/pallas_call | solution.py:258
  68.4 1.3 collective-permute-start.39
  69.7 0.2 collective-permute-start.30
  70.0 4.0 %collective-permute-start.29 = (f32[7,288,128]{2,1,0:T(8,128)}, f32[7,288,128]{2,1,0:T(8,128)}, u32[]{:S(2)}, u32[]{:S(2)}) collective-permute-start(f32[7,288,128]{2,1,0:T(8,128)} %get-tuple-element.237.refs_0_.refs_1_), channel_id=1, source_target_pairs={{0,8},{8,0},{16,24},{24,16},{1,9},{9,1},{17,25},{25,17},{2,10},{10... | collective-permute-start | bytes 3096584 | tf_op jit(solution)/shard_map/ppermute | solution.py:681
  74.0 7.1 %collective-permute-done.36.refs_4_.refs_5_ = f32[6,288,128]{2,1,0:T(8,128)} collective-permute-done((f32[6,288,128]{2,1,0:T(8,128)}, f32[6,288,128]{2,1,0:T(8,128)}, u32[]{:S(2)}, u32[]{:S(2)}) %collective-permute-start.36) | collective-permute-done | bytes 884768 | tf_op jit(solution)/shard_map/ppermute | solution.py:680
  81.2 7.7 %collective-permute-start.38 = (f32[8,288,128]{2,1,0:T(8,128)}, f32[8,288,128]{2,1,0:T(8,128)}, u32[]{:S(2)}, u32[]{:S(2)}) collective-permute-start(f32[8,288,128]{2,1,0:T(8,128)} %propagate.6.refs_0_), channel_id=1, source_target_pairs={{0,8},{8,0},{16,24},{24,16},{1,9},{9,1},{17,25},{25,17},{2,10},{10... | collective-permute-start | bytes 3538952 | tf_op jit(solution)/shard_map/ppermute | solution.py:681
  88.9 21.7 %pack.2 = (f32[7,288,128]{2,1,0:T(8,128)}, f32[6,288,128]{2,1,0:T(8,128)}, f32[4,288,128]{2,1,0:T(8,128)}, f32[4,288,128]{2,1,0:T(8,128)}, f32[4,288,128]{2,1,0:T(8,128)}) custom-call(s32[64]{0:T(128)} %slice_reduce_fusion.group_ref, f32[8,36,64,128]{3,2,1,0:T(8,128)} %bitcast.17, f32[8,36,64,128]{3,2,1,0:T(8,128)} %bitcast.18, s32[64,128]{1,0:T(8,128)S(1)} %copy-done.1, ...), custom_call_target="tpu_custom_call" | custom-call | tf_op jit(solution)/shard_map/pack/pallas_call | solution.py:476
  110.5 0.3 collective-permute-start.27
  110.8 17.7 %collective-permute-done.30.refs_4_.refs_5_ = f32[7,288,128]{2,1,0:T(8,128)} collective-permute-done((f32[7,288,128]{2,1,0:T(8,128)}, f32[7,288,128]{2,1,0:T(8,128)}, u32[]{:S(2)}, u32[]{:S(2)}) %collective-permute-start.30) | collective-permute-done | bytes 1032224 | tf_op jit(solution)/shard_map/ppermute | solution.py:680
  128.6 7.6 %collective-permute-start.26 = (f32[4,288,128]{2,1,0:T(8,128)}, f32[4,288,128]{2,1,0:T(8,128)S(1)}, u32[]{:S(2)}, u32[]{:S(2)}) collective-permute-start(f32[4,288,128]{2,1,0:T(8,128)} %get-tuple-element.236.refs_0_.refs_1_), channel_id=1, source_target_pairs={{0,8},{8,0},{16,24},{24,16},{1,9},{9,1},{17,25},{25,17},{2,10},{10... | collective-permute-start | bytes 1769480 | tf_op jit(solution)/shard_map/ppermute | solution.py:681
  136.2 0.2 collective-permute-start.15
  136.4 0.3 collective-permute-start.14
  136.7 1.2 collective-permute-start.18
  138.0 3.1 %collective-permute-done.27.refs_4_.refs_5_ = f32[4,288,128]{2,1,0:T(8,128)S(1)} collective-permute-done((f32[4,288,128]{2,1,0:T(8,128)}, f32[4,288,128]{2,1,0:T(8,128)S(1)}, u32[]{:S(2)}, u32[]{:S(2)}) %collective-permute-start.27) | collective-permute-done | bytes 589856 | tf_op jit(solution)/shard_map/ppermute | solution.py:680
  141.1 0.2 collective-permute-start.21
  141.3 7.9 %collective-permute-start.17 = (f32[4,288,128]{2,1,0:T(8,128)}, f32[4,288,128]{2,1,0:T(8,128)S(1)}, u32[]{:S(2)}, u32[]{:S(2)}) collective-permute-start(f32[4,288,128]{2,1,0:T(8,128)} %get-tuple-element.233.refs_0_.refs_1_), channel_id=1, source_target_pairs={{0,8},{8,0},{16,24},{24,16},{1,9},{9,1},{17,25},{25,17},{2,10},{10... | collective-permute-start | bytes 1769480 | tf_op jit(solution)/shard_map/ppermute | solution.py:681
  149.2 4.5 %collective-permute-done.15.refs_4_.refs_5_ = f32[4,288,128]{2,1,0:T(8,128)S(1)} collective-permute-done((f32[4,288,128]{2,1,0:T(8,128)}, f32[4,288,128]{2,1,0:T(8,128)S(1)}, u32[]{:S(2)}, u32[]{:S(2)}) %collective-permute-start.15) | collective-permute-done | bytes 589856 | tf_op jit(solution)/shard_map/ppermute | solution.py:680
  153.7 0.2 collective-permute-start.24
  154.0 7.9 %collective-permute-start.34 = (f32[6,288,128]{2,1,0:T(8,128)}, f32[6,288,128]{2,1,0:T(8,128)}, u32[]{:S(2)}, u32[]{:S(2)}) collective-permute-start(f32[6,288,128]{2,1,0:T(8,128)} %copy-done.4), channel_id=1, source_target_pairs={{0,8},{8,0},{16,24},{24,16},{1,9},{9,1},{17,25},{25,17},{2,10},{10... | collective-permute-start | bytes 2654216 | tf_op jit(solution)/shard_map/ppermute | solution.py:684
  161.9 4.5 %collective-permute-done.18.refs_4_.refs_5_ = f32[4,288,128]{2,1,0:T(8,128)S(1)} collective-permute-done((f32[4,288,128]{2,1,0:T(8,128)}, f32[4,288,128]{2,1,0:T(8,128)S(1)}, u32[]{:S(2)}, u32[]{:S(2)}) %collective-permute-start.18) | collective-permute-done | bytes 589856 | tf_op jit(solution)/shard_map/ppermute | solution.py:680
  166.4 7.6 %collective-permute-start.37 = (f32[6,288,128]{2,1,0:T(8,128)}, f32[6,288,128]{2,1,0:T(8,128)}, u32[]{:S(2)}, u32[]{:S(2)}) collective-permute-start(f32[6,288,128]{2,1,0:T(8,128)} %collective-permute-done.36.refs_4_.refs_5_), channel_id=1, source_target_pairs={{0,8},{8,0},{16,24},{24,16},{1,9},{9,1},{17,25},{25,17},{2,10},{10... | collective-permute-start | bytes 2654216 | tf_op jit(solution)/shard_map/ppermute | solution.py:684
  174.1 33.5 %collective-permute-done.24.refs_4_.refs_5_ = f32[6,288,128]{2,1,0:T(8,128)} collective-permute-done((f32[6,288,128]{2,1,0:T(8,128)}, f32[6,288,128]{2,1,0:T(8,128)}, u32[]{:S(2)}, u32[]{:S(2)}) %collective-permute-start.24) | collective-permute-done | bytes 884768 | tf_op jit(solution)/shard_map/ppermute | solution.py:680
  207.6 4.0 %collective-permute-start.28 = (f32[4,288,128]{2,1,0:T(8,128)S(1)}, f32[4,288,128]{2,1,0:T(8,128)S(1)}, u32[]{:S(2)}, u32[]{:S(2)}) collective-permute-start(f32[4,288,128]{2,1,0:T(8,128)S(1)} %collective-permute-done.27.refs_4_.refs_5_), channel_id=1, source_target_pairs={{0,8},{8,0},{16,24},{24,16},{1,9},{9,1},{17,25},{25,17},{2,10},{10... | collective-permute-start | bytes 1769480 | tf_op jit(solution)/shard_map/ppermute | solution.py:684
  211.7 0.4 collective-permute-start.19
  212.2 1.0 collective-permute-done.28.refs_6_.refs_7_
  213.2 0.4 collective-permute-start.20
  213.6 0.5 collective-permute-done.16.refs_6_.refs_7_
  214.1 0.4 collective-permute-start.22
  214.4 0.5 collective-permute-done.19.refs_6_.refs_7_
  214.9 0.4 collective-permute-start.23
  215.3 0.5 copy-done.12
  215.8 0.4 collective-permute-start.25
  216.1 0.8 dynamic_slice.3
  217.0 0.5 slice.6
  218.0 0.1 broadcast_in_dim.6.refs_10_.refs_6_
  218.1 0.2 broadcast_in_dim.7.refs_11_.refs_7_
  218.4 6.5 %packed_sources.14.refs_1_ = f32[6,288,128]{2,1,0:T(8,128)} custom-call(s32[4]{0:T(128)S(1)} %pad_add_fusion.where_ref, f32[6,288,128]{2,1,0:T(8,128)} %get-tuple-element.238.refs_0_.refs_1_, f32[6,288,128]{2,1,0:T(8,128)} %get-tuple-element.238.refs_0_.refs_1_, f32[6,288,128]{2,1,0:T(8,128)} %collective-permute-done.32.refs_2_.refs_3_, ...), custom_call_target="tpu_custom_call" | custom-call | tf_op jit(solution)/shard_map/packed_sources/pallas_call | solution.py:558
  224.8 6.2 %packed_sources.15.refs_2_ = f32[6,288,128]{2,1,0:T(8,128)} custom-call(s32[4]{0:T(128)S(1)} %pad_add_fusion.where_ref, f32[6,288,128]{2,1,0:T(8,128)} %get-tuple-element.239.refs_0_.refs_1_, f32[6,288,128]{2,1,0:T(8,128)} %get-tuple-element.239.refs_0_.refs_1_, f32[6,288,128]{2,1,0:T(8,128)} %collective-permute-done.35.refs_2_.refs_3_, ...), custom_call_target="tpu_custom_call" | custom-call | tf_op jit(solution)/shard_map/packed_sources/pallas_call | solution.py:558
  231.0 4.8 %packed_sources.8.refs_3_.refs_0_ = f32[4,288,128]{2,1,0:T(8,128)} custom-call(s32[4]{0:T(128)S(1)} %pad_add_fusion.where_ref, f32[4,288,128]{2,1,0:T(8,128)} %get-tuple-element.230.refs_0_.refs_1_, f32[4,288,128]{2,1,0:T(8,128)} %get-tuple-element.230.refs_0_.refs_1_, f32[4,288,128]{2,1,0:T(8,128)} %copy-done.9, f32[4,288,128]{2,1,0:T(8,128)} %copy-done.9, ...), custom_call_target="tpu_custom_call" | custom-call | tf_op jit(solution)/shard_map/packed_sources/pallas_call | solution.py:558
  235.8 4.8 %packed_sources.12.refs_2_ = f32[4,288,128]{2,1,0:T(8,128)} custom-call(s32[4]{0:T(128)S(1)} %pad_add_fusion.where_ref, f32[4,288,128]{2,1,0:T(8,128)} %get-tuple-element.236.refs_0_.refs_1_, f32[4,288,128]{2,1,0:T(8,128)} %get-tuple-element.236.refs_0_.refs_1_, f32[4,288,128]{2,1,0:T(8,128)} %copy-done.6, f32[4,288,128]{2,1,0:T(8,128)} %copy-done.6, ...), custom_call_target="tpu_custom_call" | custom-call | tf_op jit(solution)/shard_map/packed_sources/pallas_call | solution.py:558
  240.6 4.8 %packed_sources.9.refs_1_ = f32[4,288,128]{2,1,0:T(8,128)} custom-call(s32[4]{0:T(128)S(1)} %pad_add_fusion.where_ref, f32[4,288,128]{2,1,0:T(8,128)} %get-tuple-element.233.refs_0_.refs_1_, f32[4,288,128]{2,1,0:T(8,128)} %get-tuple-element.233.refs_0_.refs_1_, f32[4,288,128]{2,1,0:T(8,128)} %copy-done.10, f32[4,288,128]{2,1,0:T(8,128)} %copy-done.10, ...), custom_call_target="tpu_custom_call" | custom-call | tf_op jit(solution)/shard_map/packed_sources/pallas_call | solution.py:558
  245.4 7.2 %packed_sources.13.refs_0_ = f32[7,288,128]{2,1,0:T(8,128)} custom-call(s32[4]{0:T(128)S(1)} %pad_add_fusion.where_ref, f32[7,288,128]{2,1,0:T(8,128)} %get-tuple-element.237.refs_0_.refs_1_, f32[7,288,128]{2,1,0:T(8,128)} %get-tuple-element.237.refs_0_.refs_1_, f32[7,288,128]{2,1,0:T(8,128)} %collective-permute-done.29.refs_2_.refs_3_, ...), custom_call_target="tpu_custom_call" | custom-call | tf_op jit(solution)/shard_map/packed_sources/pallas_call | solution.py:558
  252.5 7.1 %sources.10.refs_4_ = f32[288,64,128]{2,1,0:T(8,128)} custom-call(s32[4]{0:T(128)S(1)} %pad_add_fusion.where_ref, s32[1]{0:T(128)} %constant.60.clone.1._, f32[8,288,128]{2,1,0:T(8,128)} %propagate.6.refs_0_, f32[8,288,128]{2,1,0:T(8,128)} %collective-permute-done.38.refs_1_, f32[8,288,128]{2,1,0:T(8,128)} %collective-permute-done.39.refs_2_, ...), custom_call_target="tpu_custom_call" | custom-call | tf_op jit(solution)/shard_map/sources/pallas_call | solution.py:327
  259.7 6.6 %spread.4.refs_4_ = f32[288,64,128]{2,1,0:T(8,128)} custom-call(s32[64]{0:T(128)} %slice_reduce_fusion.group_ref, f32[7,288,128]{2,1,0:T(8,128)} %packed_sources.13.refs_0_, f32[6,288,128]{2,1,0:T(8,128)} %packed_sources.14.refs_1_, f32[6,288,128]{2,1,0:T(8,128)} %packed_sources.15.refs_2_, ...), custom_call_target="tpu_custom_call", output_to_operand_aliasing={{}: (5, {})} | custom-call | tf_op jit(solution)/shard_map/spread/pallas_call | solution.py:619
  266.2 6.2 %packed_sources.11.refs_1_ = f32[6,288,128]{2,1,0:T(8,128)} custom-call(s32[4]{0:T(128)S(1)} %pad_add_fusion.where_ref, f32[6,288,128]{2,1,0:T(8,128)} %get-tuple-element.235.refs_0_.refs_1_, f32[6,288,128]{2,1,0:T(8,128)} %get-tuple-element.235.refs_0_.refs_1_, f32[6,288,128]{2,1,0:T(8,128)} %collective-permute-done.23.refs_2_.refs_3_, ...), custom_call_target="tpu_custom_call" | custom-call | tf_op jit(solution)/shard_map/packed_sources/pallas_call | solution.py:558
  272.5 7.1 %packed_sources.10.refs_0_ = f32[7,288,128]{2,1,0:T(8,128)} custom-call(s32[4]{0:T(128)S(1)} %pad_add_fusion.where_ref, f32[7,288,128]{2,1,0:T(8,128)} %get-tuple-element.234.refs_0_.refs_1_, f32[7,288,128]{2,1,0:T(8,128)} %get-tuple-element.234.refs_0_.refs_1_, f32[7,288,128]{2,1,0:T(8,128)} %collective-permute-done.20.refs_2_.refs_3_, ...), custom_call_target="tpu_custom_call" | custom-call | tf_op jit(solution)/shard_map/packed_sources/pallas_call | solution.py:558
  279.6 5.4 %spread.5.refs_5_ = f32[288,64,128]{2,1,0:T(8,128)} custom-call(s32[64]{0:T(128)} %slice_reduce_fusion.group_ref, f32[7,288,128]{2,1,0:T(8,128)} %packed_sources.10.refs_0_, f32[6,288,128]{2,1,0:T(8,128)} %packed_sources.11.refs_1_, f32[4,288,128]{2,1,0:T(8,128)} %packed_sources.12.refs_2_, ...), custom_call_target="tpu_custom_call", output_to_operand_aliasing={{}: (5, {})} | custom-call | tf_op jit(solution)/shard_map/spread/pallas_call | solution.py:619
  285.0 4.9 %spread.6.refs_3_ = f32[288,64,128]{2,1,0:T(8,128)} custom-call(s32[64]{0:T(128)} %slice_reduce_fusion.group_ref, f32[7,288,128]{2,1,0:T(8,128)} %packed_sources.10.refs_0_, f32[6,288,128]{2,1,0:T(8,128)} %packed_sources.11.refs_1_, f32[4,288,128]{2,1,0:T(8,128)} %packed_sources.12.refs_2_, ...), custom_call_target="tpu_custom_call", output_to_operand_aliasing={{}: (6, {})} | custom-call | tf_op jit(solution)/shard_map/spread/pallas_call | solution.py:619
  289.9 3.9 %spread.7 = f32[288,64,128]{2,1,0:T(8,128)} custom-call(s32[64]{0:T(128)} %slice_reduce_fusion.group_ref, f32[4,288,128]{2,1,0:T(8,128)} %packed_sources.8.refs_3_.refs_0_, f32[4,288,128]{2,1,0:T(8,128)} %packed_sources.9.refs_1_, s32[64,128]{1,0:T(8,128)} %get-tuple-element.229.refs_9_.refs_5_.refs_3_.refs_4_.refs_2_, ...), custom_call_target="tpu_custom_call", output_to_operand_aliasing={{}: (4, {})} | custom-call | tf_op jit(solution)/shard_map/spread/pallas_call | solution.py:619
  (62 shorter events, 0.5 us)
Async XLA Ops:
  3.2 18.7 %copy-start.1 = (s32[64,128]{1,0:T(8,128)S(1)}, s32[64,128]{1,0:T(8,128)}, u32[]{:S(2)}) copy-start(s32[64,128]{1,0:T(8,128)} %refs_8_.17) | copy-start | bytes 98308
  19.6 10.5 %copy-start.16 = (s32[8,128]{1,0:T(8,128)S(1)}, s32[8,128]{1,0:T(8,128)}, u32[]{:S(2)}) copy-start(s32[8,128]{1,0:T(8,128)} %get-tuple-element.225) | copy-start | bytes 12292
  19.6 43.4 %copy-start.14 = (f32[2,36]{1,0:T(2,128)S(1)}, f32[2,36]{1,0:T(2,128)}, u32[]{:S(2)}) copy-start(f32[2,36]{1,0:T(2,128)} %constant.61.clone.refs_10_.refs_6_.refs_5_) | copy-start | bytes 868
  19.6 50.3 %collective-permute-start.33 = (f32[6,288,128]{2,1,0:T(8,128)}, f32[6,288,128]{2,1,0:T(8,128)S(1)}, u32[]{:S(2)}, u32[]{:S(2)}) collective-permute-start(f32[6,288,128]{2,1,0:T(8,128)} %get-tuple-element.238.refs_0_.refs_1_), channel_id=1, source_target_pairs={{0,16},{8,24},{16,0},{24,8},{1,17},{9,25},{17,1},{25,9},{2,18},{10... | collective-permute-start | bytes 2654216 | tf_op jit(solution)/shard_map/ppermute | solution.py:680
  20.9 53.0 %collective-permute-start.32 = (f32[6,288,128]{2,1,0:T(8,128)}, f32[6,288,128]{2,1,0:T(8,128)}, u32[]{:S(2)}, u32[]{:S(2)}) collective-permute-start(f32[6,288,128]{2,1,0:T(8,128)} %get-tuple-element.238.refs_0_.refs_1_), channel_id=1, source_target_pairs={{0,8},{8,0},{16,24},{24,16},{1,9},{9,1},{17,25},{25,17},{2,10},{10... | collective-permute-start | bytes 2654216 | tf_op jit(solution)/shard_map/ppermute | solution.py:681
  24.8 43.6 %collective-permute-start.12 = (f32[4,296,128]{2,1,0:T(8,128)}, f32[4,296,128]{2,1,0:T(8,128)S(1)}, u32[]{:S(2)}, u32[]{:S(2)}) collective-permute-start(f32[4,296,128]{2,1,0:T(8,128)} %get-tuple-element.227), channel_id=1, source_target_pairs={{0,1},{1,2},{2,3},{3,4},{4,5},{5,6},{6,7},{8,9},{9,10},{10,11},{11... | collective-permute-start | bytes 1818632 | tf_op jit(solution)/shard_map/ppermute | solution.py:692
  27.9 41.8 %collective-permute-start.13 = (f32[4,296,128]{2,1,0:T(8,128)}, f32[4,296,128]{2,1,0:T(8,128)S(1)}, u32[]{:S(2)}, u32[]{:S(2)}) collective-permute-start(f32[4,296,128]{2,1,0:T(8,128)} %get-tuple-element.228), channel_id=1, source_target_pairs={{1,0},{2,1},{3,2},{4,3},{5,4},{6,5},{7,6},{9,8},{10,9},{11,10},{12... | collective-permute-start | bytes 1818632 | tf_op jit(solution)/shard_map/ppermute | solution.py:693
  30.1 25.1 %collective-permute-start.9 = (s32[8,128]{1,0:T(8,128)S(1)}, s32[8,128]{1,0:T(8,128)S(1)}, u32[]{:S(2)}, u32[]{:S(2)}) collective-permute-start(s32[8,128]{1,0:T(8,128)S(1)} %copy-done.16), channel_id=1, source_target_pairs={{0,1},{1,2},{2,3},{3,4},{4,5},{5,6},{6,7},{7,0},{8,9},{9,10},{10,1... | collective-permute-start | bytes 12296 | tf_op jit(solution)/shard_map/ppermute | solution.py:697
  55.2 4.3 %collective-permute-start.10 = (s32[8,128]{1,0:T(8,128)S(1)}, s32[8,128]{1,0:T(8,128)S(1)}, u32[]{:S(2)}, u32[]{:S(2)}) collective-permute-start(s32[8,128]{1,0:T(8,128)S(1)} %max.9), channel_id=1, source_target_pairs={{0,2},{1,3},{2,4},{3,5},{4,6},{5,7},{6,0},{7,1},{8,10},{9,11},{10,... | collective-permute-start | bytes 12296 | tf_op jit(solution)/shard_map/ppermute | solution.py:697
  59.4 3.4 %collective-permute-start.11 = (s32[8,128]{1,0:T(8,128)S(1)}, s32[8,128]{1,0:T(8,128)S(1)}, u32[]{:S(2)}, u32[]{:S(2)}) collective-permute-start(s32[8,128]{1,0:T(8,128)S(1)} %max.10), channel_id=1, source_target_pairs={{0,4},{1,5},{2,6},{3,7},{4,0},{5,1},{6,2},{7,3},{8,12},{9,13},{10,... | collective-permute-start | bytes 12296 | tf_op jit(solution)/shard_map/ppermute | solution.py:697
  62.8 18.4 %collective-permute-start.36 = (f32[6,288,128]{2,1,0:T(8,128)}, f32[6,288,128]{2,1,0:T(8,128)}, u32[]{:S(2)}, u32[]{:S(2)}) collective-permute-start(f32[6,288,128]{2,1,0:T(8,128)} %get-tuple-element.239.refs_0_.refs_1_), channel_id=1, source_target_pairs={{0,16},{8,24},{16,0},{24,8},{1,17},{9,25},{17,1},{25,9},{2,18},{10... | collective-permute-start | bytes 2654216 | tf_op jit(solution)/shard_map/ppermute | solution.py:680
  68.4 12.8 %copy-start.2 = (f32[4,296,128]{2,1,0:T(8,128)}, f32[4,296,128]{2,1,0:T(8,128)S(1)}, u32[]{:S(2)}) copy-start(f32[4,296,128]{2,1,0:T(8,128)S(1)} %collective-permute-done.12.refs_5_.refs_6_) | copy-start | bytes 1818628
  68.4 68.0 %collective-permute-start.39 = (f32[8,288,128]{2,1,0:T(8,128)}, f32[8,288,128]{2,1,0:T(8,128)}, u32[]{:S(2)}, u32[]{:S(2)}) collective-permute-start(f32[8,288,128]{2,1,0:T(8,128)} %propagate.6.refs_0_), channel_id=1, source_target_pairs={{0,16},{8,24},{16,0},{24,8},{1,17},{9,25},{17,1},{25,9},{2,18},{10... | collective-permute-start | bytes 3538952 | tf_op jit(solution)/shard_map/ppermute | solution.py:680
  69.7 11.5 %copy-start.3 = (f32[4,296,128]{2,1,0:T(8,128)}, f32[4,296,128]{2,1,0:T(8,128)S(1)}, u32[]{:S(2)}) copy-start(f32[4,296,128]{2,1,0:T(8,128)S(1)} %collective-permute-done.13.refs_7_.refs_8_) | copy-start | bytes 1818628
  69.7 148.4 %copy-start.15 = (f32[1152]{0:T(1024)S(1)}, f32[1152]{0:T(1024)}, u32[]{:S(2)}) copy-start(f32[1152]{0:T(1024)} %param.18) | copy-start | bytes 13828
  69.7 58.8 %collective-permute-start.30 = (f32[7,288,128]{2,1,0:T(8,128)}, f32[7,288,128]{2,1,0:T(8,128)}, u32[]{:S(2)}, u32[]{:S(2)}) collective-permute-start(f32[7,288,128]{2,1,0:T(8,128)} %get-tuple-element.237.refs_0_.refs_1_), channel_id=1, source_target_pairs={{0,16},{8,24},{16,0},{24,8},{1,17},{9,25},{17,1},{25,9},{2,18},{10... | collective-permute-start | bytes 3096584 | tf_op jit(solution)/shard_map/ppermute | solution.py:680
  70.0 11.2 %copy-start.4 = (f32[6,288,128]{2,1,0:T(8,128)}, f32[6,288,128]{2,1,0:T(8,128)S(1)}, u32[]{:S(2)}) copy-start(f32[6,288,128]{2,1,0:T(8,128)S(1)} %collective-permute-done.33.refs_4_.refs_5_) | copy-start | bytes 2654212
  70.0 66.2 %collective-permute-start.29 = (f32[7,288,128]{2,1,0:T(8,128)}, f32[7,288,128]{2,1,0:T(8,128)}, u32[]{:S(2)}, u32[]{:S(2)}) collective-permute-start(f32[7,288,128]{2,1,0:T(8,128)} %get-tuple-element.237.refs_0_.refs_1_), channel_id=1, source_target_pairs={{0,8},{8,0},{16,24},{24,16},{1,9},{9,1},{17,25},{25,17},{2,10},{10... | collective-permute-start | bytes 3096584 | tf_op jit(solution)/shard_map/ppermute | solution.py:681
  74.0 36.6 %collective-permute-start.35 = (f32[6,288,128]{2,1,0:T(8,128)}, f32[6,288,128]{2,1,0:T(8,128)}, u32[]{:S(2)}, u32[]{:S(2)}) collective-permute-start(f32[6,288,128]{2,1,0:T(8,128)} %get-tuple-element.239.refs_0_.refs_1_), channel_id=1, source_target_pairs={{0,8},{8,0},{16,24},{24,16},{1,9},{9,1},{17,25},{25,17},{2,10},{10... | collective-permute-start | bytes 2654216 | tf_op jit(solution)/shard_map/ppermute | solution.py:681
  81.2 55.5 %collective-permute-start.38 = (f32[8,288,128]{2,1,0:T(8,128)}, f32[8,288,128]{2,1,0:T(8,128)}, u32[]{:S(2)}, u32[]{:S(2)}) collective-permute-start(f32[8,288,128]{2,1,0:T(8,128)} %propagate.6.refs_0_), channel_id=1, source_target_pairs={{0,8},{8,0},{16,24},{24,16},{1,9},{9,1},{17,25},{25,17},{2,10},{10... | collective-permute-start | bytes 3538952 | tf_op jit(solution)/shard_map/ppermute | solution.py:681
  88.9 129.5 %copy-start = (bf16[1152,1152]{1,0:T(8,128)(2,1)S(1)}, bf16[1152,1152]{1,0:T(8,128)(2,1)}, u32[]{:S(2)}) copy-start(bf16[1152,1152]{1,0:T(8,128)(2,1)} %refs_4_.7) | copy-start | bytes 7962628
  110.5 30.6 %collective-permute-start.27 = (f32[4,288,128]{2,1,0:T(8,128)}, f32[4,288,128]{2,1,0:T(8,128)S(1)}, u32[]{:S(2)}, u32[]{:S(2)}) collective-permute-start(f32[4,288,128]{2,1,0:T(8,128)} %get-tuple-element.236.refs_0_.refs_1_), channel_id=1, source_target_pairs={{0,16},{8,24},{16,0},{24,8},{1,17},{9,25},{17,1},{25,9},{2,18},{10... | collective-permute-start | bytes 1769480 | tf_op jit(solution)/shard_map/ppermute | solution.py:680
  128.6 12.8 %collective-permute-start.26 = (f32[4,288,128]{2,1,0:T(8,128)}, f32[4,288,128]{2,1,0:T(8,128)S(1)}, u32[]{:S(2)}, u32[]{:S(2)}) collective-permute-start(f32[4,288,128]{2,1,0:T(8,128)} %get-tuple-element.236.refs_0_.refs_1_), channel_id=1, source_target_pairs={{0,8},{8,0},{16,24},{24,16},{1,9},{9,1},{17,25},{25,17},{2,10},{10... | collective-permute-start | bytes 1769480 | tf_op jit(solution)/shard_map/ppermute | solution.py:681
  136.2 17.5 %collective-permute-start.15 = (f32[4,288,128]{2,1,0:T(8,128)}, f32[4,288,128]{2,1,0:T(8,128)S(1)}, u32[]{:S(2)}, u32[]{:S(2)}) collective-permute-start(f32[4,288,128]{2,1,0:T(8,128)} %get-tuple-element.230.refs_0_.refs_1_), channel_id=1, source_target_pairs={{0,16},{8,24},{16,0},{24,8},{1,17},{9,25},{17,1},{25,9},{2,18},{10... | collective-permute-start | bytes 1769480 | tf_op jit(solution)/shard_map/ppermute | solution.py:680
  136.4 17.5 %collective-permute-start.14 = (f32[4,288,128]{2,1,0:T(8,128)}, f32[4,288,128]{2,1,0:T(8,128)S(1)}, u32[]{:S(2)}, u32[]{:S(2)}) collective-permute-start(f32[4,288,128]{2,1,0:T(8,128)} %get-tuple-element.230.refs_0_.refs_1_), channel_id=1, source_target_pairs={{0,8},{8,0},{16,24},{24,16},{1,9},{9,1},{17,25},{25,17},{2,10},{10... | collective-permute-start | bytes 1769480 | tf_op jit(solution)/shard_map/ppermute | solution.py:681
  136.7 29.7 %collective-permute-start.18 = (f32[4,288,128]{2,1,0:T(8,128)}, f32[4,288,128]{2,1,0:T(8,128)S(1)}, u32[]{:S(2)}, u32[]{:S(2)}) collective-permute-start(f32[4,288,128]{2,1,0:T(8,128)} %get-tuple-element.233.refs_0_.refs_1_), channel_id=1, source_target_pairs={{0,16},{8,24},{16,0},{24,8},{1,17},{9,25},{17,1},{25,9},{2,18},{10... | collective-permute-start | bytes 1769480 | tf_op jit(solution)/shard_map/ppermute | solution.py:680
  141.1 66.5 %copy-start.5 = (f32[4,288,128]{2,1,0:T(8,128)}, f32[4,288,128]{2,1,0:T(8,128)S(1)}, u32[]{:S(2)}) copy-start(f32[4,288,128]{2,1,0:T(8,128)S(1)} %collective-permute-done.27.refs_4_.refs_5_) | copy-start | bytes 1769476
  141.1 70.5 %collective-permute-start.21 = (f32[7,288,128]{2,1,0:T(8,128)}, f32[7,288,128]{2,1,0:T(8,128)}, u32[]{:S(2)}, u32[]{:S(2)}) collective-permute-start(f32[7,288,128]{2,1,0:T(8,128)} %get-tuple-element.234.refs_0_.refs_1_), channel_id=1, source_target_pairs={{0,16},{8,24},{16,0},{24,8},{1,17},{9,25},{17,1},{25,9},{2,18},{10... | collective-permute-start | bytes 3096584 | tf_op jit(solution)/shard_map/ppermute | solution.py:680
  141.3 71.9 %copy-start.6 = (f32[4,288,128]{2,1,0:T(8,128)}, f32[4,288,128]{2,1,0:T(8,128)S(1)}, u32[]{:S(2)}) copy-start(f32[4,288,128]{2,1,0:T(8,128)S(1)} %collective-permute-done.26.refs_2_.refs_3_) | copy-start | bytes 1769476
  141.3 32.7 %collective-permute-start.17 = (f32[4,288,128]{2,1,0:T(8,128)}, f32[4,288,128]{2,1,0:T(8,128)S(1)}, u32[]{:S(2)}, u32[]{:S(2)}) collective-permute-start(f32[4,288,128]{2,1,0:T(8,128)} %get-tuple-element.233.refs_0_.refs_1_), channel_id=1, source_target_pairs={{0,8},{8,0},{16,24},{24,16},{1,9},{9,1},{17,25},{25,17},{2,10},{10... | collective-permute-start | bytes 1769480 | tf_op jit(solution)/shard_map/ppermute | solution.py:681
  153.7 59.9 %copy-start.7 = (f32[4,288,128]{2,1,0:T(8,128)}, f32[4,288,128]{2,1,0:T(8,128)S(1)}, u32[]{:S(2)}) copy-start(f32[4,288,128]{2,1,0:T(8,128)S(1)} %collective-permute-done.15.refs_4_.refs_5_) | copy-start | bytes 1769476
  153.7 53.8 %collective-permute-start.24 = (f32[6,288,128]{2,1,0:T(8,128)}, f32[6,288,128]{2,1,0:T(8,128)}, u32[]{:S(2)}, u32[]{:S(2)}) collective-permute-start(f32[6,288,128]{2,1,0:T(8,128)} %get-tuple-element.235.refs_0_.refs_1_), channel_id=1, source_target_pairs={{0,16},{8,24},{16,0},{24,8},{1,17},{9,25},{17,1},{25,9},{2,18},{10... | collective-permute-start | bytes 2654216 | tf_op jit(solution)/shard_map/ppermute | solution.py:680
  154.0 60.9 %copy-start.9 = (f32[4,288,128]{2,1,0:T(8,128)}, f32[4,288,128]{2,1,0:T(8,128)S(1)}, u32[]{:S(2)}) copy-start(f32[4,288,128]{2,1,0:T(8,128)S(1)} %collective-permute-done.14.refs_2_.refs_3_) | copy-start | bytes 1769476
  154.0 57.7 %collective-permute-start.34 = (f32[6,288,128]{2,1,0:T(8,128)}, f32[6,288,128]{2,1,0:T(8,128)}, u32[]{:S(2)}, u32[]{:S(2)}) collective-permute-start(f32[6,288,128]{2,1,0:T(8,128)} %copy-done.4), channel_id=1, source_target_pairs={{0,8},{8,0},{16,24},{24,16},{1,9},{9,1},{17,25},{25,17},{2,10},{10... | collective-permute-start | bytes 2654216 | tf_op jit(solution)/shard_map/ppermute | solution.py:684
  166.4 47.7 %copy-start.8 = (f32[4,288,128]{2,1,0:T(8,128)}, f32[4,288,128]{2,1,0:T(8,128)S(1)}, u32[]{:S(2)}) copy-start(f32[4,288,128]{2,1,0:T(8,128)S(1)} %collective-permute-done.18.refs_4_.refs_5_) | copy-start | bytes 1769476
  166.4 45.7 %collective-permute-start.37 = (f32[6,288,128]{2,1,0:T(8,128)}, f32[6,288,128]{2,1,0:T(8,128)}, u32[]{:S(2)}, u32[]{:S(2)}) collective-permute-start(f32[6,288,128]{2,1,0:T(8,128)} %collective-permute-done.36.refs_4_.refs_5_), channel_id=1, source_target_pairs={{0,8},{8,0},{16,24},{24,16},{1,9},{9,1},{17,25},{25,17},{2,10},{10... | collective-permute-start | bytes 2654216 | tf_op jit(solution)/shard_map/ppermute | solution.py:684
  174.0 41.3 %copy-start.10 = (f32[4,288,128]{2,1,0:T(8,128)}, f32[4,288,128]{2,1,0:T(8,128)S(1)}, u32[]{:S(2)}) copy-start(f32[4,288,128]{2,1,0:T(8,128)S(1)} %collective-permute-done.17.refs_2_.refs_3_) | copy-start | bytes 1769476
  174.0 41.3 %collective-permute-start.31 = (f32[7,288,128]{2,1,0:T(8,128)}, f32[7,288,128]{2,1,0:T(8,128)}, u32[]{:S(2)}, u32[]{:S(2)}) collective-permute-start(f32[7,288,128]{2,1,0:T(8,128)} %collective-permute-done.30.refs_4_.refs_5_), channel_id=1, source_target_pairs={{0,8},{8,0},{16,24},{24,16},{1,9},{9,1},{17,25},{25,17},{2,10},{10... | collective-permute-start | bytes 3096584 | tf_op jit(solution)/shard_map/ppermute | solution.py:684
  207.6 5.6 %collective-permute-start.28 = (f32[4,288,128]{2,1,0:T(8,128)S(1)}, f32[4,288,128]{2,1,0:T(8,128)S(1)}, u32[]{:S(2)}, u32[]{:S(2)}) collective-permute-start(f32[4,288,128]{2,1,0:T(8,128)S(1)} %collective-permute-done.27.refs_4_.refs_5_), channel_id=1, source_target_pairs={{0,8},{8,0},{16,24},{24,16},{1,9},{9,1},{17,25},{25,17},{2,10},{10... | collective-permute-start | bytes 1769480 | tf_op jit(solution)/shard_map/ppermute | solution.py:684
  211.6 2.5 collective-permute-start.16
  211.7 3.2 %collective-permute-start.19 = (f32[4,288,128]{2,1,0:T(8,128)S(1)}, f32[4,288,128]{2,1,0:T(8,128)S(1)}, u32[]{:S(2)}, u32[]{:S(2)}) collective-permute-start(f32[4,288,128]{2,1,0:T(8,128)S(1)} %collective-permute-done.18.refs_4_.refs_5_), channel_id=1, source_target_pairs={{0,8},{8,0},{16,24},{24,16},{1,9},{9,1},{17,25},{25,17},{2,10},{10... | collective-permute-start | bytes 1769480 | tf_op jit(solution)/shard_map/ppermute | solution.py:684
  212.1 40.4 %collective-permute-start.40 = (f32[8,288,128]{2,1,0:T(8,128)}, f32[8,288,128]{2,1,0:T(8,128)}, u32[]{:S(2)}, u32[]{:S(2)}) collective-permute-start(f32[8,288,128]{2,1,0:T(8,128)} %collective-permute-done.39.refs_2_), channel_id=1, source_target_pairs={{0,8},{8,0},{16,24},{24,16},{1,9},{9,1},{17,25},{25,17},{2,10},{10... | collective-permute-start | bytes 3538952 | tf_op jit(solution)/shard_map/ppermute | solution.py:684
  213.2 2.1 copy-start.11
  213.2 59.2 %collective-permute-start.20 = (f32[7,288,128]{2,1,0:T(8,128)}, f32[7,288,128]{2,1,0:T(8,128)}, u32[]{:S(2)}, u32[]{:S(2)}) collective-permute-start(f32[7,288,128]{2,1,0:T(8,128)} %get-tuple-element.234.refs_0_.refs_1_), channel_id=1, source_target_pairs={{0,8},{8,0},{16,24},{24,16},{1,9},{9,1},{17,25},{25,17},{2,10},{10... | collective-permute-start | bytes 3096584 | tf_op jit(solution)/shard_map/ppermute | solution.py:681
  214.1 1.2 copy-start.13
  214.1 58.4 %collective-permute-start.22 = (f32[7,288,128]{2,1,0:T(8,128)}, f32[7,288,128]{2,1,0:T(8,128)}, u32[]{:S(2)}, u32[]{:S(2)}) collective-permute-start(f32[7,288,128]{2,1,0:T(8,128)} %collective-permute-done.21.refs_4_.refs_5_), channel_id=1, source_target_pairs={{0,8},{8,0},{16,24},{24,16},{1,9},{9,1},{17,25},{25,17},{2,10},{10... | collective-permute-start | bytes 3096584 | tf_op jit(solution)/shard_map/ppermute | solution.py:684
  214.9 0.8 copy-start.12
  214.9 51.3 %collective-permute-start.23 = (f32[6,288,128]{2,1,0:T(8,128)}, f32[6,288,128]{2,1,0:T(8,128)}, u32[]{:S(2)}, u32[]{:S(2)}) collective-permute-start(f32[6,288,128]{2,1,0:T(8,128)} %get-tuple-element.235.refs_0_.refs_1_), channel_id=1, source_target_pairs={{0,8},{8,0},{16,24},{24,16},{1,9},{9,1},{17,25},{25,17},{2,10},{10... | collective-permute-start | bytes 2654216 | tf_op jit(solution)/shard_map/ppermute | solution.py:681
  215.8 50.5 %collective-permute-start.25 = (f32[6,288,128]{2,1,0:T(8,128)}, f32[6,288,128]{2,1,0:T(8,128)}, u32[]{:S(2)}, u32[]{:S(2)}) collective-permute-start(f32[6,288,128]{2,1,0:T(8,128)} %collective-permute-done.24.refs_4_.refs_5_), channel_id=1, source_target_pairs={{0,8},{8,0},{16,24},{24,16},{1,9},{9,1},{17,25},{25,17},{2,10},{10... | collective-permute-start | bytes 2654216 | tf_op jit(solution)/shard_map/ppermute | solution.py:684
where the time goes:
time: 295 us; the launch traced here: 294 us
  Pallas kernels  123 us (42%)
  waiting for transfers between devices  101 us (34%)
  starting transfers between devices  64.8 us (22%)
  local copies, waits for them, and re-layouts  3.51 us (1%)
    ppermute x9, waiting for transfers between devices, exchange(): far = [lax.ppermute(piece, 'bins', s) for s in shifts]  70.5 us
    pallas_call x8, Pallas kernels, packed_sources(): pl.pallas_call(functools.partial(packed_sources_kernel, count, size), gri...  47.5 us
    pallas_call x2, Pallas kernels, pack(): pl.pallas_call(functools.partial(pack_kernel, edge, blocks, packed, cells...  38.1 us
    ppermute x9, starting transfers between devices, exchange(): near = lax.ppermute(piece, 'bins', partner)  29.3 us
    ppermute x3, waiting for transfers between devices, local(): over = jnp.maximum(over, lax.ppermute(over, 'space', ring))  28.7 us
    ppermute x9, starting transfers between devices, exchange(): parts += [came_in, lax.ppermute(came_in, 'bins', partner)]  21 us
    pallas_call x4, Pallas kernels, spread(): pl.pallas_call(functools.partial(spread_kernel, base, packed, skip), grid...  20.7 us
    pallas_call x1, Pallas kernels, add_sources(): pl.pallas_call(functools.partial(source_kernel, count, out is not None),...  7.12 us
  transfers between devices with their start and end apart: 32, of which 12 were waited for; matrix products, arithmetic and copies ran while one was open for 1% of the time, Pallas kernels for 29%

commit v1 on v0

--- a/solution.py
+++ b/solution.py
@@ -389,6 +389,14 @@
     return pl.pallas_call(plan_kernel, out_shape=[table, table, small], name="plan")(land_mask, *tables)
 
 
+def ballot_kernel(in_ref, out_ref):
+    out_ref[...] = in_ref[...]
+
+
+def ballot(over):
+    return pl.pallas_call(ballot_kernel, out_shape=jax.ShapeDtypeStruct(over.shape, over.dtype), name="ballot")(over)
+
+
 def listed(blocks):
     def at(i, *_):
         block = blocks[0]
@@ -691,6 +699,7 @@
     head, tail = edges(spectra, land_mask)
     before = lax.ppermute(tail, "space", [(n, n + 1) for n in range(slabs - 1)])
     after = lax.ppermute(head, "space", [(n + 1, n) for n in range(slabs - 1)])
+    over = ballot(over)
     reach = 1
     while reach < slabs:
         ring = [(n, (n + reach) % slabs) for n in range(slabs)]

time: 295 us -> 296 us (level)
  no operation moved by 1% of the time
where the time goes in v1:
time: 296 us; the launch traced here: 295 us
  Pallas kernels  125 us (42%)
  waiting for transfers between devices  99.9 us (34%)
  starting transfers between devices  64.7 us (22%)
  local copies, waits for them, and re-layouts  3.61 us (1%)
    ppermute x9, waiting for transfers between devices, exchange(): far = [lax.ppermute(piece, 'bins', s) for s in shifts]  70.4 us
    pallas_call x8, Pallas kernels, packed_sources(): pl.pallas_call(functools.partial(packed_sources_kernel, count, size), gri...  47.5 us
    pallas_call x2, Pallas kernels, pack(): pl.pallas_call(functools.partial(pack_kernel, edge, blocks, packed, cells...  38.1 us
    ppermute x9, starting transfers between devices, exchange(): near = lax.ppermute(piece, 'bins', partner)  29.3 us
    ppermute x3, waiting for transfers between devices, local(): over = jnp.maximum(over, lax.ppermute(over, 'space', ring))  27.5 us
    ppermute x9, starting transfers between devices, exchange(): parts += [came_in, lax.ppermute(came_in, 'bins', partner)]  21 us
    pallas_call x4, Pallas kernels, spread(): pl.pallas_call(functools.partial(spread_kernel, base, packed, skip), grid...  20.7 us
    pallas_call x1, Pallas kernels, add_sources(): pl.pallas_call(functools.partial(source_kernel, count, out is not None),...  7.12 us
  transfers between devices with their start and end apart: 32, of which 12 were waited for; matrix products, arithmetic and copies ran while one was open for 1% of the time, Pallas kernels for 29%

profile of v1, /device:TPU:3, one launch (start us, length us, event | category | flops | bytes accessed | tf_op | source)
XLA Modules:
  0.0 294.6 jit_solution(1548845915724544879)
XLA Ops:
  0.0 1.7 plan.1
  1.7 1.4 slice_reduce_fusion.group_ref
  3.2 16.5 %pack.3 = (f32[7,288,128]{2,1,0:T(8,128)}, f32[6,288,128]{2,1,0:T(8,128)}, f32[6,288,128]{2,1,0:T(8,128)}) custom-call(s32[64]{0:T(128)} %slice_reduce_fusion.group_ref, f32[8,36,64,128]{3,2,1,0:T(8,128)} %bitcast.13, f32[8,36,64,128]{3,2,1,0:T(8,128)} %bitcast.14, s32[64,128]{1,0:T(8,128)} %refs_8_.17, s32[64,128]{1,0:T(8,128)} %refs_8_.17, ...), custom_call_target="tpu_custom_call" | custom-call | tf_op jit(solution)/shard_map/pack/pallas_call | solution.py:484
  19.6 1.2 collective-permute-start.33
  20.9 1.0 collective-permute-start.32
  21.8 2.9 edges.1
  24.7 3.2 %collective-permute-start.12 = (f32[4,296,128]{2,1,0:T(8,128)}, f32[4,296,128]{2,1,0:T(8,128)S(1)}, u32[]{:S(2)}, u32[]{:S(2)}) collective-permute-start(f32[4,296,128]{2,1,0:T(8,128)} %get-tuple-element.227), channel_id=1, source_target_pairs={{0,1},{1,2},{2,3},{3,4},{4,5},{5,6},{6,7},{8,9},{9,10},{10,11},{11... | collective-permute-start | bytes 1818632 | tf_op jit(solution)/shard_map/ppermute | solution.py:700
  27.9 2.1 collective-permute-start.13
  30.0 1.3 ballot.1
  31.3 2.1 collective-permute-start.9
  33.4 21.7 %collective-permute-done.9 = s32[8,128]{1,0:T(8,128)S(1)} collective-permute-done((s32[8,128]{1,0:T(8,128)}, s32[8,128]{1,0:T(8,128)S(1)}, u32[]{:S(2)}, u32[]{:S(2)}) %collective-permute-start.9) | collective-permute-done | bytes 4128 | tf_op jit(solution)/shard_map/ppermute | solution.py:706
  55.1 0.7 max.9
  55.8 1.3 collective-permute-start.10
  57.1 3.0 %collective-permute-done.10 = s32[8,128]{1,0:T(8,128)S(1)} collective-permute-done((s32[8,128]{1,0:T(8,128)S(1)}, s32[8,128]{1,0:T(8,128)S(1)}, u32[]{:S(2)}, u32[]{:S(2)}) %collective-permute-start.10) | collective-permute-done | bytes 4128 | tf_op jit(solution)/shard_map/ppermute | solution.py:706
  60.1 0.5 collective-permute-start.11
  60.6 2.8 collective-permute-done.11
  63.4 0.2 collective-permute-start.36
  63.6 5.4 %propagate.6.refs_0_ = f32[8,288,128]{2,1,0:T(8,128)} custom-call(s32[1]{0:T(128)} %constant.60.clone.1._, f32[8,36,64,128]{3,2,1,0:T(8,128)} %bitcast.15, f32[8,36,64,128]{3,2,1,0:T(8,128)} %bitcast.16, s32[64,128]{1,0:T(8,128)S(1)} %copy-done.1, s32[64,128]{1,0:T(8,128)S(1)} %copy-done.1, s32[64,128]{1,0:T(8,128)S(1)} %copy-done.1, ...), custom_call_target="tpu_custom_call" | custom-call | tf_op jit(solution)/shard_map/propagate/pallas_call | solution.py:258
  69.0 1.3 collective-permute-start.39
  70.3 0.2 collective-permute-start.30
  70.6 4.0 %collective-permute-start.29 = (f32[7,288,128]{2,1,0:T(8,128)}, f32[7,288,128]{2,1,0:T(8,128)}, u32[]{:S(2)}, u32[]{:S(2)}) collective-permute-start(f32[7,288,128]{2,1,0:T(8,128)} %get-tuple-element.237.refs_0_.refs_1_), channel_id=1, source_target_pairs={{0,8},{8,0},{16,24},{24,16},{1,9},{9,1},{17,25},{25,17},{2,10},{10... | collective-permute-start | bytes 3096584 | tf_op jit(solution)/shard_map/ppermute | solution.py:689
  74.7 7.1 %collective-permute-done.36.refs_4_.refs_5_ = f32[6,288,128]{2,1,0:T(8,128)} collective-permute-done((f32[6,288,128]{2,1,0:T(8,128)}, f32[6,288,128]{2,1,0:T(8,128)}, u32[]{:S(2)}, u32[]{:S(2)}) %collective-permute-start.36) | collective-permute-done | bytes 884768 | tf_op jit(solution)/shard_map/ppermute | solution.py:688
  81.8 7.7 %collective-permute-start.38 = (f32[8,288,128]{2,1,0:T(8,128)}, f32[8,288,128]{2,1,0:T(8,128)}, u32[]{:S(2)}, u32[]{:S(2)}) collective-permute-start(f32[8,288,128]{2,1,0:T(8,128)} %propagate.6.refs_0_), channel_id=1, source_target_pairs={{0,8},{8,0},{16,24},{24,16},{1,9},{9,1},{17,25},{25,17},{2,10},{10... | collective-permute-start | bytes 3538952 | tf_op jit(solution)/shard_map/ppermute | solution.py:689
  89.5 21.7 %pack.2 = (f32[7,288,128]{2,1,0:T(8,128)}, f32[6,288,128]{2,1,0:T(8,128)}, f32[4,288,128]{2,1,0:T(8,128)}, f32[4,288,128]{2,1,0:T(8,128)}, f32[4,288,128]{2,1,0:T(8,128)}) custom-call(s32[64]{0:T(128)} %slice_reduce_fusion.group_ref, f32[8,36,64,128]{3,2,1,0:T(8,128)} %bitcast.17, f32[8,36,64,128]{3,2,1,0:T(8,128)} %bitcast.18, s32[64,128]{1,0:T(8,128)S(1)} %copy-done.1, ...), custom_call_target="tpu_custom_call" | custom-call | tf_op jit(solution)/shard_map/pack/pallas_call | solution.py:484
  111.2 0.3 collective-permute-start.27
  111.5 17.7 %collective-permute-done.30.refs_4_.refs_5_ = f32[7,288,128]{2,1,0:T(8,128)} collective-permute-done((f32[7,288,128]{2,1,0:T(8,128)}, f32[7,288,128]{2,1,0:T(8,128)}, u32[]{:S(2)}, u32[]{:S(2)}) %collective-permute-start.30) | collective-permute-done | bytes 1032224 | tf_op jit(solution)/shard_map/ppermute | solution.py:688
  129.2 7.6 %collective-permute-start.26 = (f32[4,288,128]{2,1,0:T(8,128)}, f32[4,288,128]{2,1,0:T(8,128)S(1)}, u32[]{:S(2)}, u32[]{:S(2)}) collective-permute-start(f32[4,288,128]{2,1,0:T(8,128)} %get-tuple-element.236.refs_0_.refs_1_), channel_id=1, source_target_pairs={{0,8},{8,0},{16,24},{24,16},{1,9},{9,1},{17,25},{25,17},{2,10},{10... | collective-permute-start | bytes 1769480 | tf_op jit(solution)/shard_map/ppermute | solution.py:689
  136.8 0.2 collective-permute-start.15
  137.0 0.3 collective-permute-start.14
  137.3 1.2 collective-permute-start.18
  138.6 3.1 %collective-permute-done.27.refs_4_.refs_5_ = f32[4,288,128]{2,1,0:T(8,128)S(1)} collective-permute-done((f32[4,288,128]{2,1,0:T(8,128)}, f32[4,288,128]{2,1,0:T(8,128)S(1)}, u32[]{:S(2)}, u32[]{:S(2)}) %collective-permute-start.27) | collective-permute-done | bytes 589856 | tf_op jit(solution)/shard_map/ppermute | solution.py:688
  141.7 0.2 collective-permute-start.21
  141.9 7.9 %collective-permute-start.17 = (f32[4,288,128]{2,1,0:T(8,128)}, f32[4,288,128]{2,1,0:T(8,128)S(1)}, u32[]{:S(2)}, u32[]{:S(2)}) collective-permute-start(f32[4,288,128]{2,1,0:T(8,128)} %get-tuple-element.233.refs_0_.refs_1_), channel_id=1, source_target_pairs={{0,8},{8,0},{16,24},{24,16},{1,9},{9,1},{17,25},{25,17},{2,10},{10... | collective-permute-start | bytes 1769480 | tf_op jit(solution)/shard_map/ppermute | solution.py:689
  149.9 4.5 %collective-permute-done.15.refs_4_.refs_5_ = f32[4,288,128]{2,1,0:T(8,128)S(1)} collective-permute-done((f32[4,288,128]{2,1,0:T(8,128)}, f32[4,288,128]{2,1,0:T(8,128)S(1)}, u32[]{:S(2)}, u32[]{:S(2)}) %collective-permute-start.15) | collective-permute-done | bytes 589856 | tf_op jit(solution)/shard_map/ppermute | solution.py:688
  154.4 0.2 collective-permute-start.24
  154.6 7.9 %collective-permute-start.34 = (f32[6,288,128]{2,1,0:T(8,128)}, f32[6,288,128]{2,1,0:T(8,128)}, u32[]{:S(2)}, u32[]{:S(2)}) collective-permute-start(f32[6,288,128]{2,1,0:T(8,128)} %copy-done.4), channel_id=1, source_target_pairs={{0,8},{8,0},{16,24},{24,16},{1,9},{9,1},{17,25},{25,17},{2,10},{10... | collective-permute-start | bytes 2654216 | tf_op jit(solution)/shard_map/ppermute | solution.py:692
  162.5 4.5 %collective-permute-done.18.refs_4_.refs_5_ = f32[4,288,128]{2,1,0:T(8,128)S(1)} collective-permute-done((f32[4,288,128]{2,1,0:T(8,128)}, f32[4,288,128]{2,1,0:T(8,128)S(1)}, u32[]{:S(2)}, u32[]{:S(2)}) %collective-permute-start.18) | collective-permute-done | bytes 589856 | tf_op jit(solution)/shard_map/ppermute | solution.py:688
  167.0 7.6 %collective-permute-start.37 = (f32[6,288,128]{2,1,0:T(8,128)}, f32[6,288,128]{2,1,0:T(8,128)}, u32[]{:S(2)}, u32[]{:S(2)}) collective-permute-start(f32[6,288,128]{2,1,0:T(8,128)} %collective-permute-done.36.refs_4_.refs_5_), channel_id=1, source_target_pairs={{0,8},{8,0},{16,24},{24,16},{1,9},{9,1},{17,25},{25,17},{2,10},{10... | collective-permute-start | bytes 2654216 | tf_op jit(solution)/shard_map/ppermute | solution.py:692
  174.7 33.5 %collective-permute-done.24.refs_4_.refs_5_ = f32[6,288,128]{2,1,0:T(8,128)} collective-permute-done((f32[6,288,128]{2,1,0:T(8,128)}, f32[6,288,128]{2,1,0:T(8,128)}, u32[]{:S(2)}, u32[]{:S(2)}) %collective-permute-start.24) | collective-permute-done | bytes 884768 | tf_op jit(solution)/shard_map/ppermute | solution.py:688
  208.2 4.0 %collective-permute-start.28 = (f32[4,288,128]{2,1,0:T(8,128)S(1)}, f32[4,288,128]{2,1,0:T(8,128)S(1)}, u32[]{:S(2)}, u32[]{:S(2)}) collective-permute-start(f32[4,288,128]{2,1,0:T(8,128)S(1)} %collective-permute-done.27.refs_4_.refs_5_), channel_id=1, source_target_pairs={{0,8},{8,0},{16,24},{24,16},{1,9},{9,1},{17,25},{25,17},{2,10},{10... | collective-permute-start | bytes 1769480 | tf_op jit(solution)/shard_map/ppermute | solution.py:692
  212.3 0.4 collective-permute-start.19
  212.8 1.0 collective-permute-done.28.refs_6_.refs_7_
  213.8 0.4 collective-permute-start.20
  214.2 0.5 collective-permute-done.16.refs_6_.refs_7_
  214.7 0.4 collective-permute-start.22
  215.1 0.5 collective-permute-done.19.refs_6_.refs_7_
  215.5 0.4 collective-permute-start.23
  215.9 0.5 copy-done.12
  216.4 0.4 collective-permute-start.25
  216.7 0.8 dynamic_slice.3
  217.6 0.6 slice.6
  219.2 6.5 %packed_sources.14.refs_1_ = f32[6,288,128]{2,1,0:T(8,128)} custom-call(s32[4]{0:T(128)S(1)} %pad_add_fusion.where_ref, f32[6,288,128]{2,1,0:T(8,128)} %get-tuple-element.238.refs_0_.refs_1_, f32[6,288,128]{2,1,0:T(8,128)} %get-tuple-element.238.refs_0_.refs_1_, f32[6,288,128]{2,1,0:T(8,128)} %collective-permute-done.32.refs_2_.refs_3_, ...), custom_call_target="tpu_custom_call" | custom-call | tf_op jit(solution)/shard_map/packed_sources/pallas_call | solution.py:566
  225.7 6.2 %packed_sources.15.refs_2_ = f32[6,288,128]{2,1,0:T(8,128)} custom-call(s32[4]{0:T(128)S(1)} %pad_add_fusion.where_ref, f32[6,288,128]{2,1,0:T(8,128)} %get-tuple-element.239.refs_0_.refs_1_, f32[6,288,128]{2,1,0:T(8,128)} %get-tuple-element.239.refs_0_.refs_1_, f32[6,288,128]{2,1,0:T(8,128)} %collective-permute-done.35.refs_2_.refs_3_, ...), custom_call_target="tpu_custom_call" | custom-call | tf_op jit(solution)/shard_map/packed_sources/pallas_call | solution.py:566
  231.9 4.8 %packed_sources.8.refs_3_.refs_0_ = f32[4,288,128]{2,1,0:T(8,128)} custom-call(s32[4]{0:T(128)S(1)} %pad_add_fusion.where_ref, f32[4,288,128]{2,1,0:T(8,128)} %get-tuple-element.230.refs_0_.refs_1_, f32[4,288,128]{2,1,0:T(8,128)} %get-tuple-element.230.refs_0_.refs_1_, f32[4,288,128]{2,1,0:T(8,128)} %copy-done.9, f32[4,288,128]{2,1,0:T(8,128)} %copy-done.9, ...), custom_call_target="tpu_custom_call" | custom-call | tf_op jit(solution)/shard_map/packed_sources/pallas_call | solution.py:566
  236.7 4.8 %packed_sources.12.refs_2_ = f32[4,288,128]{2,1,0:T(8,128)} custom-call(s32[4]{0:T(128)S(1)} %pad_add_fusion.where_ref, f32[4,288,128]{2,1,0:T(8,128)} %get-tuple-element.236.refs_0_.refs_1_, f32[4,288,128]{2,1,0:T(8,128)} %get-tuple-element.236.refs_0_.refs_1_, f32[4,288,128]{2,1,0:T(8,128)} %copy-done.6, f32[4,288,128]{2,1,0:T(8,128)} %copy-done.6, ...), custom_call_target="tpu_custom_call" | custom-call | tf_op jit(solution)/shard_map/packed_sources/pallas_call | solution.py:566
  241.4 4.8 %packed_sources.9.refs_1_ = f32[4,288,128]{2,1,0:T(8,128)} custom-call(s32[4]{0:T(128)S(1)} %pad_add_fusion.where_ref, f32[4,288,128]{2,1,0:T(8,128)} %get-tuple-element.233.refs_0_.refs_1_, f32[4,288,128]{2,1,0:T(8,128)} %get-tuple-element.233.refs_0_.refs_1_, f32[4,288,128]{2,1,0:T(8,128)} %copy-done.10, f32[4,288,128]{2,1,0:T(8,128)} %copy-done.10, ...), custom_call_target="tpu_custom_call" | custom-call | tf_op jit(solution)/shard_map/packed_sources/pallas_call | solution.py:566
  246.2 7.1 %packed_sources.13.refs_0_ = f32[7,288,128]{2,1,0:T(8,128)} custom-call(s32[4]{0:T(128)S(1)} %pad_add_fusion.where_ref, f32[7,288,128]{2,1,0:T(8,128)} %get-tuple-element.237.refs_0_.refs_1_, f32[7,288,128]{2,1,0:T(8,128)} %get-tuple-element.237.refs_0_.refs_1_, f32[7,288,128]{2,1,0:T(8,128)} %collective-permute-done.29.refs_2_.refs_3_, ...), custom_call_target="tpu_custom_call" | custom-call | tf_op jit(solution)/shard_map/packed_sources/pallas_call | solution.py:566
  253.4 7.1 %sources.10.refs_4_ = f32[288,64,128]{2,1,0:T(8,128)} custom-call(s32[4]{0:T(128)S(1)} %pad_add_fusion.where_ref, s32[1]{0:T(128)} %constant.60.clone.1._, f32[8,288,128]{2,1,0:T(8,128)} %propagate.6.refs_0_, f32[8,288,128]{2,1,0:T(8,128)} %collective-permute-done.38.refs_1_, f32[8,288,128]{2,1,0:T(8,128)} %collective-permute-done.39.refs_2_, ...), custom_call_target="tpu_custom_call" | custom-call | tf_op jit(solution)/shard_map/sources/pallas_call | solution.py:327
  260.5 6.6 %spread.4.refs_4_ = f32[288,64,128]{2,1,0:T(8,128)} custom-call(s32[64]{0:T(128)} %slice_reduce_fusion.group_ref, f32[7,288,128]{2,1,0:T(8,128)} %packed_sources.13.refs_0_, f32[6,288,128]{2,1,0:T(8,128)} %packed_sources.14.refs_1_, f32[6,288,128]{2,1,0:T(8,128)} %packed_sources.15.refs_2_, ...), custom_call_target="tpu_custom_call", output_to_operand_aliasing={{}: (5, {})} | custom-call | tf_op jit(solution)/shard_map/spread/pallas_call | solution.py:627
  267.0 6.2 %packed_sources.11.refs_1_ = f32[6,288,128]{2,1,0:T(8,128)} custom-call(s32[4]{0:T(128)S(1)} %pad_add_fusion.where_ref, f32[6,288,128]{2,1,0:T(8,128)} %get-tuple-element.235.refs_0_.refs_1_, f32[6,288,128]{2,1,0:T(8,128)} %get-tuple-element.235.refs_0_.refs_1_, f32[6,288,128]{2,1,0:T(8,128)} %collective-permute-done.23.refs_2_.refs_3_, ...), custom_call_target="tpu_custom_call" | custom-call | tf_op jit(solution)/shard_map/packed_sources/pallas_call | solution.py:566
  273.3 7.1 %packed_sources.10.refs_0_ = f32[7,288,128]{2,1,0:T(8,128)} custom-call(s32[4]{0:T(128)S(1)} %pad_add_fusion.where_ref, f32[7,288,128]{2,1,0:T(8,128)} %get-tuple-element.234.refs_0_.refs_1_, f32[7,288,128]{2,1,0:T(8,128)} %get-tuple-element.234.refs_0_.refs_1_, f32[7,288,128]{2,1,0:T(8,128)} %collective-permute-done.20.refs_2_.refs_3_, ...), custom_call_target="tpu_custom_call" | custom-call | tf_op jit(solution)/shard_map/packed_sources/pallas_call | solution.py:566
  280.4 5.4 %spread.5.refs_5_ = f32[288,64,128]{2,1,0:T(8,128)} custom-call(s32[64]{0:T(128)} %slice_reduce_fusion.group_ref, f32[7,288,128]{2,1,0:T(8,128)} %packed_sources.10.refs_0_, f32[6,288,128]{2,1,0:T(8,128)} %packed_sources.11.refs_1_, f32[4,288,128]{2,1,0:T(8,128)} %packed_sources.12.refs_2_, ...), custom_call_target="tpu_custom_call", output_to_operand_aliasing={{}: (5, {})} | custom-call | tf_op jit(solution)/shard_map/spread/pallas_call | solution.py:627
  285.8 4.9 %spread.6.refs_3_ = f32[288,64,128]{2,1,0:T(8,128)} custom-call(s32[64]{0:T(128)} %slice_reduce_fusion.group_ref, f32[7,288,128]{2,1,0:T(8,128)} %packed_sources.10.refs_0_, f32[6,288,128]{2,1,0:T(8,128)} %packed_sources.11.refs_1_, f32[4,288,128]{2,1,0:T(8,128)} %packed_sources.12.refs_2_, ...), custom_call_target="tpu_custom_call", output_to_operand_aliasing={{}: (6, {})} | custom-call | tf_op jit(solution)/shard_map/spread/pallas_call | solution.py:627
  290.7 3.9 %spread.7 = f32[288,64,128]{2,1,0:T(8,128)} custom-call(s32[64]{0:T(128)} %slice_reduce_fusion.group_ref, f32[4,288,128]{2,1,0:T(8,128)} %packed_sources.8.refs_3_.refs_0_, f32[4,288,128]{2,1,0:T(8,128)} %packed_sources.9.refs_1_, s32[64,128]{1,0:T(8,128)} %get-tuple-element.229.refs_9_.refs_5_.refs_3_.refs_4_.refs_2_, ...), custom_call_target="tpu_custom_call", output_to_operand_aliasing={{}: (4, {})} | custom-call | tf_op jit(solution)/shard_map/spread/pallas_call | solution.py:627
  (61 shorter events, 0.8 us)
Async XLA Ops:
  3.2 18.7 %copy-start.1 = (s32[64,128]{1,0:T(8,128)S(1)}, s32[64,128]{1,0:T(8,128)}, u32[]{:S(2)}) copy-start(s32[64,128]{1,0:T(8,128)} %refs_8_.17) | copy-start | bytes 98308
  19.6 44.0 %copy-start.14 = (f32[2,36]{1,0:T(2,128)S(1)}, f32[2,36]{1,0:T(2,128)}, u32[]{:S(2)}) copy-start(f32[2,36]{1,0:T(2,128)} %constant.61.clone.refs_10_.refs_6_.refs_5_) | copy-start | bytes 868
  19.6 51.0 %collective-permute-start.33 = (f32[6,288,128]{2,1,0:T(8,128)}, f32[6,288,128]{2,1,0:T(8,128)S(1)}, u32[]{:S(2)}, u32[]{:S(2)}) collective-permute-start(f32[6,288,128]{2,1,0:T(8,128)} %get-tuple-element.238.refs_0_.refs_1_), channel_id=1, source_target_pairs={{0,16},{8,24},{16,0},{24,8},{1,17},{9,25},{17,1},{25,9},{2,18},{10... | collective-permute-start | bytes 2654216 | tf_op jit(solution)/shard_map/ppermute | solution.py:688
  20.9 53.7 %collective-permute-start.32 = (f32[6,288,128]{2,1,0:T(8,128)}, f32[6,288,128]{2,1,0:T(8,128)}, u32[]{:S(2)}, u32[]{:S(2)}) collective-permute-start(f32[6,288,128]{2,1,0:T(8,128)} %get-tuple-element.238.refs_0_.refs_1_), channel_id=1, source_target_pairs={{0,8},{8,0},{16,24},{24,16},{1,9},{9,1},{17,25},{25,17},{2,10},{10... | collective-permute-start | bytes 2654216 | tf_op jit(solution)/shard_map/ppermute | solution.py:689
  24.7 44.3 %collective-permute-start.12 = (f32[4,296,128]{2,1,0:T(8,128)}, f32[4,296,128]{2,1,0:T(8,128)S(1)}, u32[]{:S(2)}, u32[]{:S(2)}) collective-permute-start(f32[4,296,128]{2,1,0:T(8,128)} %get-tuple-element.227), channel_id=1, source_target_pairs={{0,1},{1,2},{2,3},{3,4},{4,5},{5,6},{6,7},{8,9},{9,10},{10,11},{11... | collective-permute-start | bytes 1818632 | tf_op jit(solution)/shard_map/ppermute | solution.py:700
  27.9 42.4 %collective-permute-start.13 = (f32[4,296,128]{2,1,0:T(8,128)}, f32[4,296,128]{2,1,0:T(8,128)S(1)}, u32[]{:S(2)}, u32[]{:S(2)}) collective-permute-start(f32[4,296,128]{2,1,0:T(8,128)} %get-tuple-element.228), channel_id=1, source_target_pairs={{1,0},{2,1},{3,2},{4,3},{5,4},{6,5},{7,6},{9,8},{10,9},{11,10},{12... | collective-permute-start | bytes 1818632 | tf_op jit(solution)/shard_map/ppermute | solution.py:701
  31.3 23.8 %collective-permute-start.9 = (s32[8,128]{1,0:T(8,128)}, s32[8,128]{1,0:T(8,128)S(1)}, u32[]{:S(2)}, u32[]{:S(2)}) collective-permute-start(s32[8,128]{1,0:T(8,128)} %ballot.1), channel_id=1, source_target_pairs={{0,1},{1,2},{2,3},{3,4},{4,5},{5,6},{6,7},{7,0},{8,9},{9,10},{10,1... | collective-permute-start | bytes 12296 | tf_op jit(solution)/shard_map/ppermute | solution.py:706
  55.8 4.3 %collective-permute-start.10 = (s32[8,128]{1,0:T(8,128)S(1)}, s32[8,128]{1,0:T(8,128)S(1)}, u32[]{:S(2)}, u32[]{:S(2)}) collective-permute-start(s32[8,128]{1,0:T(8,128)S(1)} %max.9), channel_id=1, source_target_pairs={{0,2},{1,3},{2,4},{3,5},{4,6},{5,7},{6,0},{7,1},{8,10},{9,11},{10,... | collective-permute-start | bytes 12296 | tf_op jit(solution)/shard_map/ppermute | solution.py:706
  60.1 3.4 %collective-permute-start.11 = (s32[8,128]{1,0:T(8,128)S(1)}, s32[8,128]{1,0:T(8,128)S(1)}, u32[]{:S(2)}, u32[]{:S(2)}) collective-permute-start(s32[8,128]{1,0:T(8,128)S(1)} %max.10), channel_id=1, source_target_pairs={{0,4},{1,5},{2,6},{3,7},{4,0},{5,1},{6,2},{7,3},{8,12},{9,13},{10,... | collective-permute-start | bytes 12296 | tf_op jit(solution)/shard_map/ppermute | solution.py:706
  63.4 18.4 %collective-permute-start.36 = (f32[6,288,128]{2,1,0:T(8,128)}, f32[6,288,128]{2,1,0:T(8,128)}, u32[]{:S(2)}, u32[]{:S(2)}) collective-permute-start(f32[6,288,128]{2,1,0:T(8,128)} %get-tuple-element.239.refs_0_.refs_1_), channel_id=1, source_target_pairs={{0,16},{8,24},{16,0},{24,8},{1,17},{9,25},{17,1},{25,9},{2,18},{10... | collective-permute-start | bytes 2654216 | tf_op jit(solution)/shard_map/ppermute | solution.py:688
  69.0 12.8 %copy-start.2 = (f32[4,296,128]{2,1,0:T(8,128)}, f32[4,296,128]{2,1,0:T(8,128)S(1)}, u32[]{:S(2)}) copy-start(f32[4,296,128]{2,1,0:T(8,128)S(1)} %collective-permute-done.12.refs_5_.refs_6_) | copy-start | bytes 1818628
  69.0 68.0 %collective-permute-start.39 = (f32[8,288,128]{2,1,0:T(8,128)}, f32[8,288,128]{2,1,0:T(8,128)}, u32[]{:S(2)}, u32[]{:S(2)}) collective-permute-start(f32[8,288,128]{2,1,0:T(8,128)} %propagate.6.refs_0_), channel_id=1, source_target_pairs={{0,16},{8,24},{16,0},{24,8},{1,17},{9,25},{17,1},{25,9},{2,18},{10... | collective-permute-start | bytes 3538952 | tf_op jit(solution)/shard_map/ppermute | solution.py:688
  70.3 11.5 %copy-start.3 = (f32[4,296,128]{2,1,0:T(8,128)}, f32[4,296,128]{2,1,0:T(8,128)S(1)}, u32[]{:S(2)}) copy-start(f32[4,296,128]{2,1,0:T(8,128)S(1)} %collective-permute-done.13.refs_7_.refs_8_) | copy-start | bytes 1818628
  70.3 148.6 %copy-start.15 = (f32[1152]{0:T(1024)S(1)}, f32[1152]{0:T(1024)}, u32[]{:S(2)}) copy-start(f32[1152]{0:T(1024)} %param.18) | copy-start | bytes 13828
  70.3 58.8 %collective-permute-start.30 = (f32[7,288,128]{2,1,0:T(8,128)}, f32[7,288,128]{2,1,0:T(8,128)}, u32[]{:S(2)}, u32[]{:S(2)}) collective-permute-start(f32[7,288,128]{2,1,0:T(8,128)} %get-tuple-element.237.refs_0_.refs_1_), channel_id=1, source_target_pairs={{0,16},{8,24},{16,0},{24,8},{1,17},{9,25},{17,1},{25,9},{2,18},{10... | collective-permute-start | bytes 3096584 | tf_op jit(solution)/shard_map/ppermute | solution.py:688
  70.6 11.2 %copy-start.4 = (f32[6,288,128]{2,1,0:T(8,128)}, f32[6,288,128]{2,1,0:T(8,128)S(1)}, u32[]{:S(2)}) copy-start(f32[6,288,128]{2,1,0:T(8,128)S(1)} %collective-permute-done.33.refs_4_.refs_5_) | copy-start | bytes 2654212
  70.6 66.2 %collective-permute-start.29 = (f32[7,288,128]{2,1,0:T(8,128)}, f32[7,288,128]{2,1,0:T(8,128)}, u32[]{:S(2)}, u32[]{:S(2)}) collective-permute-start(f32[7,288,128]{2,1,0:T(8,128)} %get-tuple-element.237.refs_0_.refs_1_), channel_id=1, source_target_pairs={{0,8},{8,0},{16,24},{24,16},{1,9},{9,1},{17,25},{25,17},{2,10},{10... | collective-permute-start | bytes 3096584 | tf_op jit(solution)/shard_map/ppermute | solution.py:689
  74.6 36.6 %collective-permute-start.35 = (f32[6,288,128]{2,1,0:T(8,128)}, f32[6,288,128]{2,1,0:T(8,128)}, u32[]{:S(2)}, u32[]{:S(2)}) collective-permute-start(f32[6,288,128]{2,1,0:T(8,128)} %get-tuple-element.239.refs_0_.refs_1_), channel_id=1, source_target_pairs={{0,8},{8,0},{16,24},{24,16},{1,9},{9,1},{17,25},{25,17},{2,10},{10... | collective-permute-start | bytes 2654216 | tf_op jit(solution)/shard_map/ppermute | solution.py:689
  81.8 55.5 %collective-permute-start.38 = (f32[8,288,128]{2,1,0:T(8,128)}, f32[8,288,128]{2,1,0:T(8,128)}, u32[]{:S(2)}, u32[]{:S(2)}) collective-permute-start(f32[8,288,128]{2,1,0:T(8,128)} %propagate.6.refs_0_), channel_id=1, source_target_pairs={{0,8},{8,0},{16,24},{24,16},{1,9},{9,1},{17,25},{25,17},{2,10},{10... | collective-permute-start | bytes 3538952 | tf_op jit(solution)/shard_map/ppermute | solution.py:689
  89.5 129.7 %copy-start = (bf16[1152,1152]{1,0:T(8,128)(2,1)S(1)}, bf16[1152,1152]{1,0:T(8,128)(2,1)}, u32[]{:S(2)}) copy-start(bf16[1152,1152]{1,0:T(8,128)(2,1)} %refs_4_.7) | copy-start | bytes 7962628
  111.2 30.5 %collective-permute-start.27 = (f32[4,288,128]{2,1,0:T(8,128)}, f32[4,288,128]{2,1,0:T(8,128)S(1)}, u32[]{:S(2)}, u32[]{:S(2)}) collective-permute-start(f32[4,288,128]{2,1,0:T(8,128)} %get-tuple-element.236.refs_0_.refs_1_), channel_id=1, source_target_pairs={{0,16},{8,24},{16,0},{24,8},{1,17},{9,25},{17,1},{25,9},{2,18},{10... | collective-permute-start | bytes 1769480 | tf_op jit(solution)/shard_map/ppermute | solution.py:688
  129.2 12.8 %collective-permute-start.26 = (f32[4,288,128]{2,1,0:T(8,128)}, f32[4,288,128]{2,1,0:T(8,128)S(1)}, u32[]{:S(2)}, u32[]{:S(2)}) collective-permute-start(f32[4,288,128]{2,1,0:T(8,128)} %get-tuple-element.236.refs_0_.refs_1_), channel_id=1, source_target_pairs={{0,8},{8,0},{16,24},{24,16},{1,9},{9,1},{17,25},{25,17},{2,10},{10... | collective-permute-start | bytes 1769480 | tf_op jit(solution)/shard_map/ppermute | solution.py:689
  136.8 17.5 %collective-permute-start.15 = (f32[4,288,128]{2,1,0:T(8,128)}, f32[4,288,128]{2,1,0:T(8,128)S(1)}, u32[]{:S(2)}, u32[]{:S(2)}) collective-permute-start(f32[4,288,128]{2,1,0:T(8,128)} %get-tuple-element.230.refs_0_.refs_1_), channel_id=1, source_target_pairs={{0,16},{8,24},{16,0},{24,8},{1,17},{9,25},{17,1},{25,9},{2,18},{10... | collective-permute-start | bytes 1769480 | tf_op jit(solution)/shard_map/ppermute | solution.py:688
  137.0 17.5 %collective-permute-start.14 = (f32[4,288,128]{2,1,0:T(8,128)}, f32[4,288,128]{2,1,0:T(8,128)S(1)}, u32[]{:S(2)}, u32[]{:S(2)}) collective-permute-start(f32[4,288,128]{2,1,0:T(8,128)} %get-tuple-element.230.refs_0_.refs_1_), channel_id=1, source_target_pairs={{0,8},{8,0},{16,24},{24,16},{1,9},{9,1},{17,25},{25,17},{2,10},{10... | collective-permute-start | bytes 1769480 | tf_op jit(solution)/shard_map/ppermute | solution.py:689
  137.3 29.7 %collective-permute-start.18 = (f32[4,288,128]{2,1,0:T(8,128)}, f32[4,288,128]{2,1,0:T(8,128)S(1)}, u32[]{:S(2)}, u32[]{:S(2)}) collective-permute-start(f32[4,288,128]{2,1,0:T(8,128)} %get-tuple-element.233.refs_0_.refs_1_), channel_id=1, source_target_pairs={{0,16},{8,24},{16,0},{24,8},{1,17},{9,25},{17,1},{25,9},{2,18},{10... | collective-permute-start | bytes 1769480 | tf_op jit(solution)/shard_map/ppermute | solution.py:688
  141.7 66.5 %copy-start.5 = (f32[4,288,128]{2,1,0:T(8,128)}, f32[4,288,128]{2,1,0:T(8,128)S(1)}, u32[]{:S(2)}) copy-start(f32[4,288,128]{2,1,0:T(8,128)S(1)} %collective-permute-done.27.refs_4_.refs_5_) | copy-start | bytes 1769476
  141.7 70.5 %collective-permute-start.21 = (f32[7,288,128]{2,1,0:T(8,128)}, f32[7,288,128]{2,1,0:T(8,128)}, u32[]{:S(2)}, u32[]{:S(2)}) collective-permute-start(f32[7,288,128]{2,1,0:T(8,128)} %get-tuple-element.234.refs_0_.refs_1_), channel_id=1, source_target_pairs={{0,16},{8,24},{16,0},{24,8},{1,17},{9,25},{17,1},{25,9},{2,18},{10... | collective-permute-start | bytes 3096584 | tf_op jit(solution)/shard_map/ppermute | solution.py:688
  141.9 71.9 %copy-start.6 = (f32[4,288,128]{2,1,0:T(8,128)}, f32[4,288,128]{2,1,0:T(8,128)S(1)}, u32[]{:S(2)}) copy-start(f32[4,288,128]{2,1,0:T(8,128)S(1)} %collective-permute-done.26.refs_2_.refs_3_) | copy-start | bytes 1769476
  141.9 32.7 %collective-permute-start.17 = (f32[4,288,128]{2,1,0:T(8,128)}, f32[4,288,128]{2,1,0:T(8,128)S(1)}, u32[]{:S(2)}, u32[]{:S(2)}) collective-permute-start(f32[4,288,128]{2,1,0:T(8,128)} %get-tuple-element.233.refs_0_.refs_1_), channel_id=1, source_target_pairs={{0,8},{8,0},{16,24},{24,16},{1,9},{9,1},{17,25},{25,17},{2,10},{10... | collective-permute-start | bytes 1769480 | tf_op jit(solution)/shard_map/ppermute | solution.py:689
  154.4 59.9 %copy-start.7 = (f32[4,288,128]{2,1,0:T(8,128)}, f32[4,288,128]{2,1,0:T(8,128)S(1)}, u32[]{:S(2)}) copy-start(f32[4,288,128]{2,1,0:T(8,128)S(1)} %collective-permute-done.15.refs_4_.refs_5_) | copy-start | bytes 1769476
  154.4 53.8 %collective-permute-start.24 = (f32[6,288,128]{2,1,0:T(8,128)}, f32[6,288,128]{2,1,0:T(8,128)}, u32[]{:S(2)}, u32[]{:S(2)}) collective-permute-start(f32[6,288,128]{2,1,0:T(8,128)} %get-tuple-element.235.refs_0_.refs_1_), channel_id=1, source_target_pairs={{0,16},{8,24},{16,0},{24,8},{1,17},{9,25},{17,1},{25,9},{2,18},{10... | collective-permute-start | bytes 2654216 | tf_op jit(solution)/shard_map/ppermute | solution.py:688
  154.6 60.9 %copy-start.9 = (f32[4,288,128]{2,1,0:T(8,128)}, f32[4,288,128]{2,1,0:T(8,128)S(1)}, u32[]{:S(2)}) copy-start(f32[4,288,128]{2,1,0:T(8,128)S(1)} %collective-permute-done.14.refs_2_.refs_3_) | copy-start | bytes 1769476
  154.6 57.7 %collective-permute-start.34 = (f32[6,288,128]{2,1,0:T(8,128)}, f32[6,288,128]{2,1,0:T(8,128)}, u32[]{:S(2)}, u32[]{:S(2)}) collective-permute-start(f32[6,288,128]{2,1,0:T(8,128)} %copy-done.4), channel_id=1, source_target_pairs={{0,8},{8,0},{16,24},{24,16},{1,9},{9,1},{17,25},{25,17},{2,10},{10... | collective-permute-start | bytes 2654216 | tf_op jit(solution)/shard_map/ppermute | solution.py:692
  167.0 47.7 %copy-start.8 = (f32[4,288,128]{2,1,0:T(8,128)}, f32[4,288,128]{2,1,0:T(8,128)S(1)}, u32[]{:S(2)}) copy-start(f32[4,288,128]{2,1,0:T(8,128)S(1)} %collective-permute-done.18.refs_4_.refs_5_) | copy-start | bytes 1769476
  167.0 45.7 %collective-permute-start.37 = (f32[6,288,128]{2,1,0:T(8,128)}, f32[6,288,128]{2,1,0:T(8,128)}, u32[]{:S(2)}, u32[]{:S(2)}) collective-permute-start(f32[6,288,128]{2,1,0:T(8,128)} %collective-permute-done.36.refs_4_.refs_5_), channel_id=1, source_target_pairs={{0,8},{8,0},{16,24},{24,16},{1,9},{9,1},{17,25},{25,17},{2,10},{10... | collective-permute-start | bytes 2654216 | tf_op jit(solution)/shard_map/ppermute | solution.py:692
  174.6 41.3 %copy-start.10 = (f32[4,288,128]{2,1,0:T(8,128)}, f32[4,288,128]{2,1,0:T(8,128)S(1)}, u32[]{:S(2)}) copy-start(f32[4,288,128]{2,1,0:T(8,128)S(1)} %collective-permute-done.17.refs_2_.refs_3_) | copy-start | bytes 1769476
  174.6 41.3 %collective-permute-start.31 = (f32[7,288,128]{2,1,0:T(8,128)}, f32[7,288,128]{2,1,0:T(8,128)}, u32[]{:S(2)}, u32[]{:S(2)}) collective-permute-start(f32[7,288,128]{2,1,0:T(8,128)} %collective-permute-done.30.refs_4_.refs_5_), channel_id=1, source_target_pairs={{0,8},{8,0},{16,24},{24,16},{1,9},{9,1},{17,25},{25,17},{2,10},{10... | collective-permute-start | bytes 3096584 | tf_op jit(solution)/shard_map/ppermute | solution.py:692
  208.2 5.6 %collective-permute-start.28 = (f32[4,288,128]{2,1,0:T(8,128)S(1)}, f32[4,288,128]{2,1,0:T(8,128)S(1)}, u32[]{:S(2)}, u32[]{:S(2)}) collective-permute-start(f32[4,288,128]{2,1,0:T(8,128)S(1)} %collective-permute-done.27.refs_4_.refs_5_), channel_id=1, source_target_pairs={{0,8},{8,0},{16,24},{24,16},{1,9},{9,1},{17,25},{25,17},{2,10},{10... | collective-permute-start | bytes 1769480 | tf_op jit(solution)/shard_map/ppermute | solution.py:692
  212.2 2.5 collective-permute-start.16
  212.3 3.2 %collective-permute-start.19 = (f32[4,288,128]{2,1,0:T(8,128)S(1)}, f32[4,288,128]{2,1,0:T(8,128)S(1)}, u32[]{:S(2)}, u32[]{:S(2)}) collective-permute-start(f32[4,288,128]{2,1,0:T(8,128)S(1)} %collective-permute-done.18.refs_4_.refs_5_), channel_id=1, source_target_pairs={{0,8},{8,0},{16,24},{24,16},{1,9},{9,1},{17,25},{25,17},{2,10},{10... | collective-permute-start | bytes 1769480 | tf_op jit(solution)/shard_map/ppermute | solution.py:692
  212.7 40.6 %collective-permute-start.40 = (f32[8,288,128]{2,1,0:T(8,128)}, f32[8,288,128]{2,1,0:T(8,128)}, u32[]{:S(2)}, u32[]{:S(2)}) collective-permute-start(f32[8,288,128]{2,1,0:T(8,128)} %collective-permute-done.39.refs_2_), channel_id=1, source_target_pairs={{0,8},{8,0},{16,24},{24,16},{1,9},{9,1},{17,25},{25,17},{2,10},{10... | collective-permute-start | bytes 3538952 | tf_op jit(solution)/shard_map/ppermute | solution.py:692
  213.8 2.1 copy-start.11
  213.8 59.4 %collective-permute-start.20 = (f32[7,288,128]{2,1,0:T(8,128)}, f32[7,288,128]{2,1,0:T(8,128)}, u32[]{:S(2)}, u32[]{:S(2)}) collective-permute-start(f32[7,288,128]{2,1,0:T(8,128)} %get-tuple-element.234.refs_0_.refs_1_), channel_id=1, source_target_pairs={{0,8},{8,0},{16,24},{24,16},{1,9},{9,1},{17,25},{25,17},{2,10},{10... | collective-permute-start | bytes 3096584 | tf_op jit(solution)/shard_map/ppermute | solution.py:689
  214.7 1.2 copy-start.13
  214.7 58.6 %collective-permute-start.22 = (f32[7,288,128]{2,1,0:T(8,128)}, f32[7,288,128]{2,1,0:T(8,128)}, u32[]{:S(2)}, u32[]{:S(2)}) collective-permute-start(f32[7,288,128]{2,1,0:T(8,128)} %collective-permute-done.21.refs_4_.refs_5_), channel_id=1, source_target_pairs={{0,8},{8,0},{16,24},{24,16},{1,9},{9,1},{17,25},{25,17},{2,10},{10... | collective-permute-start | bytes 3096584 | tf_op jit(solution)/shard_map/ppermute | solution.py:692
  215.5 0.9 copy-start.12
  215.5 51.5 %collective-permute-start.23 = (f32[6,288,128]{2,1,0:T(8,128)}, f32[6,288,128]{2,1,0:T(8,128)}, u32[]{:S(2)}, u32[]{:S(2)}) collective-permute-start(f32[6,288,128]{2,1,0:T(8,128)} %get-tuple-element.235.refs_0_.refs_1_), channel_id=1, source_target_pairs={{0,8},{8,0},{16,24},{24,16},{1,9},{9,1},{17,25},{25,17},{2,10},{10... | collective-permute-start | bytes 2654216 | tf_op jit(solution)/shard_map/ppermute | solution.py:689
  216.4 50.7 %collective-permute-start.25 = (f32[6,288,128]{2,1,0:T(8,128)}, f32[6,288,128]{2,1,0:T(8,128)}, u32[]{:S(2)}, u32[]{:S(2)}) collective-permute-start(f32[6,288,128]{2,1,0:T(8,128)} %collective-permute-done.24.refs_4_.refs_5_), channel_id=1, source_target_pairs={{0,8},{8,0},{16,24},{24,16},{1,9},{9,1},{17,25},{25,17},{2,10},{10... | collective-permute-start | bytes 2654216 | tf_op jit(solution)/shard_map/ppermute | solution.py:692
